TPU v7x, 768 devices: a whole 4x8x12 slice. The times are simulated.
768 devices in a mesh: dp: 96 (over z, y), ep: 8 (over x, core).
Axes of the slice: x: 4, y: 8, z: 12, core: 2. Of those that a mesh axis runs over, the one named last changes fastest.
Arguments:
- grad: float32 [2, 1536, 3584], P(None, 'dp', 'ep'), may hold values from -40 to 40
- momentum: float32 [2, 1536, 3584], P(None, 'dp', 'ep'), may hold values from -6 to 6
- lengths: int32 [2, 96], replicated, may hold values from 1 to 16, 1024 in all within a row
Outputs:
- new_momentum: float32 [2, 1536, 3584], P(None, 'dp', 'ep')
- update: float32 [2, 1536, 3584], P(None, 'dp', 'ep')
Inputs may be any that keep to these rules, and one draw needn't show every extreme that they name: lengths[j, d] counts the rows of matrix j held by dp index d, in order of d, in the first slots of its block of 16 slots; each row of lengths sums to 1024 and reaches 16.
All inputs are finite; a program needn't handle non-finite values.
Results may differ from a plain program's by a relative error of at most 0.009.
Values may be sent and summed in bfloat16 or wider, within the bound.
No kernel may reach another device: no remote copies, remote signals or barrier semaphores. Data moves between devices by JAX's collectives and lax.ppermute only.
A program may use at most 32 MiB of HBM per device.

v0:
```python
import math

import jax
import jax.numpy as jnp
from jax import lax
from jax.sharding import PartitionSpec as P

H = 1024
D = 3584


MOMENTUM_COEF = 0.95
EPSILON = 1e-06
FIRST_LIN = 3.0
FIRST_CUBE = -2.5
SECOND_LIN = 1.5
SECOND_CUBE = -0.5


def from_root(block, axis, owner):
    block = jnp.where(lax.axis_index(axis) == owner, block, jnp.zeros_like(block))
    return lax.psum(block, axis)


def newton_polar(scaled_gram, factor, matrix):
    product = jnp.dot(scaled_gram, matrix, preferred_element_type=jnp.float32)
    first_iter = (factor * (FIRST_LIN * matrix.astype(jnp.float32) + FIRST_CUBE * product)).astype(
        jnp.bfloat16
    )
    product = jnp.dot(scaled_gram, first_iter, preferred_element_type=jnp.float32)
    applied = (FIRST_LIN * first_iter.astype(jnp.float32) + FIRST_CUBE * product).astype(
        jnp.bfloat16
    )
    second = jnp.dot(scaled_gram, applied, preferred_element_type=jnp.float32).astype(jnp.bfloat16)
    third = FIRST_LIN * second.astype(jnp.float32) + FIRST_CUBE * jnp.dot(
        scaled_gram, second, preferred_element_type=jnp.float32
    )
    return (SECOND_LIN * first_iter.astype(jnp.float32) + SECOND_CUBE * third).astype(jnp.bfloat16)


def body(grad, momentum, lengths):
    matrices = grad.shape[0]
    slot_rows = grad.shape[1]
    columns = grad.shape[2]
    new_momentum = MOMENTUM_COEF * momentum + grad
    rounded = (grad + MOMENTUM_COEF * new_momentum).astype(jnp.bfloat16)
    holders = lax.axis_size("dp")
    myself = lax.axis_index("dp")
    is_owner = myself < matrices
    chosen = jnp.minimum(myself, matrices - 1)
    offsets = jnp.cumsum(lengths, axis=1) - lengths
    chosen_len = lax.dynamic_index_in_dim(lengths, chosen, 0, keepdims=False)
    chosen_off = lax.dynamic_index_in_dim(offsets, chosen, 0, keepdims=False)
    device_ids = jnp.arange(holders, dtype=jnp.int32)
    portion = lax.all_gather(rounded, "dp", axis=1, tiled=True)
    piece_rows = portion.shape[1]
    incoming = lax.dynamic_index_in_dim(portion, chosen, 0, keepdims=False)
    slot_ids = jnp.arange(piece_rows, dtype=jnp.int32)
    source = slot_ids // slot_rows
    within = slot_ids % slot_rows
    matches = source[:, None] == device_ids[None, :]
    length_at = jnp.sum(jnp.where(matches, chosen_len[None, :], 0), axis=1)
    offset_at = jnp.sum(jnp.where(matches, chosen_off[None, :], 0), axis=1)
    keep = jnp.logical_and(within < length_at, is_owner)
    target = jnp.where(keep, offset_at + within, H)
    matrix = jnp.zeros((H, columns), jnp.bfloat16).at[target].set(incoming, mode="drop")
    partial_value = jnp.dot(matrix, matrix.T, preferred_element_type=jnp.float32)
    gram_rows = lax.psum_scatter(partial_value, "ep", scatter_dimension=0, tiled=True)
    total_sq = lax.psum(jnp.sum(gram_rows * gram_rows), "ep")
    scale_sq = lax.rsqrt(total_sq + EPSILON)
    scaled_gram = lax.all_gather(
        (scale_sq * gram_rows).astype(jnp.bfloat16), "ep", axis=0, tiled=True
    )
    ortho = newton_polar(scaled_gram, jnp.sqrt(scale_sq), matrix)
    scale_out = math.sqrt(max(H, D))
    positions = jnp.arange(slot_rows, dtype=jnp.int32)
    results = []
    for matrix_id in range(matrices):
        owned_ortho = from_root(ortho, "dp", matrix_id)
        own_length = lax.dynamic_index_in_dim(lengths[matrix_id], myself, 0, keepdims=False)
        own_offset = lax.dynamic_index_in_dim(offsets[matrix_id], myself, 0, keepdims=False)
        is_valid = positions < own_length
        picked = jnp.take(owned_ortho, jnp.where(is_valid, own_offset + positions, 0), axis=0)
        results.append(
            jnp.where(is_valid[:, None], picked.astype(jnp.float32) * scale_out, jnp.float32(0.0))
        )
    return (new_momentum, jnp.stack(results))


def solution(mesh):
    return jax.shard_map(
        body,
        mesh=mesh,
        in_specs=(P(None, "dp", "ep"), P(None, "dp", "ep"), P()),
        out_specs=(P(None, "dp", "ep"), P(None, "dp", "ep")),
        check_vma=False,
    )
```

profile of v0, /device:TPU:1, one launch (start us, length us, event | category | flops | bytes accessed | tf_op | source)
XLA Modules:
  0.0 512.6 jit_solution(535055593706750871)
XLA Ops:
  7.2 0.0 all-gather.3.cloned.1.call-start
  7.2 1.5 add_convert_fusion
  8.7 0.0 all-gather.3.cloned.1.call-update
  8.8 0.0 reduce-scatter.2.cloned.1.call-start
  8.8 0.9 reduce_window_sum.11
  9.8 0.7 sub.12
  10.5 0.8 fusion.21
  11.3 0.2 select_reduce_fusion.1
  11.5 125.7 %all-gather.3.cloned.1.call-done = bf16[2,1536,448]{2,1,0:T(8,128)(2,1)} async-done(((bf16[2,16,448]{2,1,0:T(8,128)(2,1)}), bf16[2,1536,448]{2,1,0:T(8,128)(2,1)}) %all-gather.3.cloned.1.call-update) | async-done | bytes 2752528 | tf_op jit(solution)/shard_map/all_gather | solution.py:55
  137.3 8.0 %scatter_custom_fusion = bf16[1024,448]{1,0:T(8,128)(2,1)S(1)} fusion(s32[1536]{0:T(1024)S(1)} %fusion.14, bf16[2,1536,448]{2,1,0:T(8,128)(2,1)} %all-gather.3.cloned.1.call-done, s32[]{:T(128)S(6)} %select_n.108, s32[]{:T(128)} %constant.81.clone.1, bf16[]{:T(256)} %constant.85.clone.1), kind=kCustom, calls=%fused_computation.10 | custom fusion | bytes 2491396 | tf_op jit(solution)/shard_map/scatter | solution.py:66
  145.3 3.2 fusion.23
  148.5 0.0 reduce-scatter.2.cloned.1.call-update
  148.5 0.0 all-gather.5.cloned.1.call-start
  148.6 48.5 %reduce-scatter.2.cloned.1.call-done = f32[128,1024]{1,0:T(8,128)} async-done(((f32[1024,1024]{1,0:T(8,128)}), f32[128,1024]{1,0:T(8,128)}) %reduce-scatter.2.cloned.1.call-update) | async-done | bytes 524304 | tf_op jit(solution)/shard_map/reduce_scatter | solution.py:68
  197.1 1.8 multiply_reduce_fusion
  198.8 14.3 %psum.21 = f32[]{:T(128)} all-reduce(f32[]{:T(128)} %multiply_reduce_fusion), channel_id=1, replica_groups=mesh['dp'=96,'ep'=8] {'ep'}, use_global_device_ids=true, to_apply=%region_6.7 | all-reduce | flops 1 | bytes 8 | tf_op jit(solution)/shard_map/psum | solution.py:69
  213.8 1.8 multiply_convert_fusion.4
  215.7 0.0 all-gather.5.cloned.1.call-update
  215.7 0.0 all-reduce.3.cloned.1.call-start
  215.7 0.5 copy.13
  216.3 32.7 %all-gather.5.cloned.1.call-done = bf16[1024,1024]{1,0:T(8,128)(2,1)} async-done(((bf16[128,1024]{1,0:T(8,128)(2,1)}), bf16[1024,1024]{1,0:T(8,128)(2,1)}) %all-gather.5.cloned.1.call-update) | async-done | bytes 2097168 | tf_op jit(solution)/shard_map/all_gather | solution.py:71
  249.0 4.0 fusion.24
  253.0 5.5 %convolution_convert_fusion = bf16[1024,448]{0,1:T(8,128)(2,1)S(1)} fusion(bf16[1024,1024]{1,0:T(8,128)(2,1)} %all-gather.5.cloned.1.call-done, f32[1024,448]{0,1:T(8,128)} %fusion.24, bf16[1024,448]{0,1:T(8,128)(2,1)S(1)} %copy.13, f32[]{:T(128)S(6)} %sqrt.3), kind=kOutput, calls=%fused_computation.13 | convolution fusion | flops 1887305728 | bytes 5767172 | tf_op jit(solution)/shard_map/dot_general | solution.py:34
  258.4 5.1 broadcast_select_fusion.1
  263.6 0.0 all-reduce.3.cloned.1.call-update
  263.6 0.6 constant_dynamic-slice_fusion.4
  264.2 0.6 constant_dynamic-slice_fusion
  264.8 0.7 constant_dynamic-slice_fusion.1
  265.4 0.7 constant_dynamic-slice_fusion.5
  266.1 0.6 iota_compare_fusion.1
  266.7 0.7 iota_compare_fusion.2
  267.4 2.6 compare_and_fusion
  270.0 232.0 %all-reduce.3.cloned.1.call-done = (bf16[1024,448]{0,1:T(8,128)(2,1)}, bf16[1024,448]{0,1:T(8,128)(2,1)}) async-done(((bf16[1024,448]{0,1:T(8,128)(2,1)}, bf16[1024,448]{0,1:T(8,128)(2,1)}), (bf16[1024,448]{0,1:T(8,128)(2,1)}, bf16[1024,448]{0,1:T(8,128)(2,1)})) %all-reduce.3.cloned.1.call-update) | async-done | bytes 1835024 | tf_op jit(solution)/shard_map/psum | solution.py:22
  502.0 0.0 copy-start
  502.0 1.5 copy.15
  503.5 0.0 copy-done
  503.5 0.5 copy.14
  504.1 0.6 gather_fusion.1
  504.7 0.6 gather_fusion
  505.3 0.1 select_bitcast_fusion
  505.3 0.1 select_bitcast_fusion.1
  505.4 0.6 pad_maximum_fusion
  (5 shorter events, 0.1 us)
Async XLA Ops:
  7.2 130.1 %all-gather.3.cloned.1.call-start = ((), (), s32[]{:S(2)}) async-start(), calls=%async_computation.1 | async-start | bytes 3178496 | tf_op jit(solution)/shard_map/all_gather | solution.py:55
  8.8 188.3 %reduce-scatter.2.cloned.1.call-start = ((), (), s32[]{:S(2)}) async-start(), calls=%async_computation.2 | async-start | bytes 4718592 | tf_op jit(solution)/shard_map/reduce_scatter | solution.py:68
  148.5 100.5 %all-gather.5.cloned.1.call-start = ((), (), s32[]{:S(2)}) async-start(), calls=%async_computation.3 | async-start | bytes 2359296 | tf_op jit(solution)/shard_map/all_gather | solution.py:71
  215.7 286.3 %all-reduce.3.cloned.1.call-start = ((), (), s32[]{:S(2)}) async-start(), calls=%async_computation.4 | async-start | bytes 3670016 | tf_op jit(solution)/shard_map/psum | solution.py:22
  502.0 1.6 copy-start
Sparse Core Ops, SparseCore 0:
  12.3 124.9 all-gather.2
  148.6 48.3 reduce-scatter.1
  215.8 33.1 all-gather.4
  263.7 238.2 all-reduce.2
where the time goes:
time: 519 us; the launch traced here: 513 us
  waiting for transfers between devices  439 us (85%)
  matrix products  17.8 us (3%)
  local copies, waits for them, and re-layouts  15 us (3%)
  between operations  14.6 us (3%)
  blocking collectives  14.3 us (3%)
  other arithmetic  11.7 us (2%)
    psum x1, waiting for transfers between devices, from_root(): return lax.psum(block, axis)  232 us
    all_gather x1, waiting for transfers between devices, body(): portion = lax.all_gather(rounded, 'dp', axis=1, tiled=True)  126 us
    reduce_scatter x1, waiting for transfers between devices, body(): lax.psum_scatter(partial_value, 'ep', scatter_dimension=0, tiled=True)  48.5 us
    all_gather x1, waiting for transfers between devices, body(): lax.all_gather((scale_sq * gram_rows).astype(jnp.bfloat16), 'ep', axis=0,...  32.7 us
    psum x1, blocking collectives, body(): total_sq = lax.psum(jnp.sum(gram_rows * gram_rows), 'ep')  14.3 us
  transfers between devices with their start and end apart: 4, of which 4 were waited for; matrix products, arithmetic and copies ran while one was open for 2% of the time, Pallas kernels for 0%

commit v1 on v0

v1 whole, which is shorter than its diff:
```python
import math

import jax
import jax.numpy as jnp
from jax import lax
from jax.sharding import Mesh
from jax.sharding import PartitionSpec as P

H = 1024
D = 3584

MOMENTUM_COEF = 0.95
EPSILON = 1e-06
FIRST_LIN = 3.0
FIRST_CUBE = -2.5
SECOND_LIN = 1.5
SECOND_CUBE = -0.5

NZ, NY, NX, NC = 12, 8, 4, 2


def spread(block, axis, size):
    return lax.all_to_all(
        jnp.broadcast_to(block[None], (size,) + block.shape), axis, 0, 0
    )


def swap(block):
    return lax.ppermute(block, "c", [(0, 1), (1, 0)])


def sum_columns(partial):
    return jnp.sum(spread(partial, "x", NX).astype(jnp.float32), axis=0)


def rows_dot_t(rows, matrix):
    return lax.dot_general(
        rows, matrix, (((1,), (1,)), ((), ())), preferred_element_type=jnp.float32
    ).astype(jnp.bfloat16)


def rows_dot(rows, matrix):
    return jnp.dot(rows.astype(jnp.bfloat16), matrix, preferred_element_type=jnp.float32)


def body(grad, momentum, lengths):
    f32, bf16 = jnp.float32, jnp.bfloat16
    new_momentum = MOMENTUM_COEF * momentum + grad
    rounded = (grad + MOMENTUM_COEF * new_momentum).astype(bf16)
    dp = lax.axis_index("z") * NY + lax.axis_index("y")
    core = lax.axis_index("c")
    own_lengths = lax.dynamic_index_in_dim(lengths, dp, 1, keepdims=False)
    slots = lax.broadcasted_iota(jnp.int32, rounded.shape, 1)
    rounded = jnp.where(slots < own_lengths[:, None, None], rounded, jnp.zeros_like(rounded))
    first_core = core == 0
    mine = jnp.where(first_core, rounded[0], rounded[1])
    theirs = jnp.where(first_core, rounded[1], rounded[0])
    rows = jnp.concatenate([mine, swap(theirs)], axis=1)
    columns = rows.shape[1]
    matrix = spread(rows, "z", NZ).reshape(-1, columns)
    matrix = lax.all_gather(matrix, "y", axis=0, tiled=True)

    gram = sum_columns(rows_dot_t(rows, matrix))
    total_sq = jnp.broadcast_to(jnp.sum(gram * gram), (8, 128))
    total_sq = jnp.sum(spread(total_sq, "z", NZ), axis=0)
    total_sq = jnp.sum(spread(total_sq, "y", NY), axis=0)[0, 0]
    scale_sq = lax.rsqrt(total_sq + EPSILON)
    factor = jnp.sqrt(scale_sq)

    first = (
        factor * (FIRST_LIN * rows.astype(f32) + FIRST_CUBE * rows_dot(scale_sq * gram, matrix))
    ).astype(bf16)
    product = rows_dot(scale_sq * sum_columns(rows_dot_t(first, matrix)), matrix)
    applied = (FIRST_LIN * first.astype(f32) + FIRST_CUBE * product).astype(bf16)
    second = rows_dot(scale_sq * sum_columns(rows_dot_t(applied, matrix)), matrix).astype(bf16)
    product = rows_dot(scale_sq * sum_columns(rows_dot_t(second, matrix)), matrix)
    third = FIRST_LIN * second.astype(f32) + FIRST_CUBE * product
    ortho = (SECOND_LIN * first.astype(f32) + SECOND_CUBE * third).astype(bf16)

    half = columns // 2
    other = swap(ortho[:, half:])
    own = ortho[:, :half]
    update = jnp.stack([jnp.where(first_core, own, other), jnp.where(first_core, other, own)])
    return (new_momentum, update.astype(f32) * math.sqrt(max(H, D)))


def solution(mesh):
    grid = Mesh(mesh.devices.reshape(NZ, NY, NX, NC), ("z", "y", "x", "c"))
    spec = P(None, ("z", "y"), ("x", "c"))
    return jax.shard_map(
        body,
        mesh=grid,
        in_specs=(spec, spec, P()),
        out_specs=(spec, spec),
        check_vma=False,
    )
```

time: 519 us -> 182 us (0.35); the launches traced: 513 us -> 182 us
  waiting for transfers between devices: 439 us -> 43.5 us
  blocking collectives: 14.3 us -> 86.6 us
  starting transfers between devices: 0.16 us -> 24.8 us
  local copies, waits for them, and re-layouts: 15 us -> 2.24 us
  matrix products: 17.8 us -> 7 us
  other arithmetic: 11.7 us -> 3 us
    psum x1 -> x0, waiting for transfers between devices: 232 us -> none  [from_root(): return lax.psum(block, axis)]
    all_gather x2 -> x1, waiting for transfers between devices: 158 us -> 41.8 us  [body(): matrix = lax.all_gather(matrix, 'y', axis=0, tiled=True)]
    all_to_all x0 -> x7, blocking collectives: none -> 86.6 us  [spread(): lax.all_to_all(jnp.broadcast_to(block[None], (size,) + block.shape), axis...]
    reduce_scatter x1 -> x0, waiting for transfers between devices: 48.5 us -> none  [body(): lax.psum_scatter(partial_value, 'ep', scatter_dimension=0, tiled=True)]
    ppermute x0 -> x2, starting transfers between devices: none -> 24.8 us  [swap(): return lax.ppermute(block, 'c', [(0, 1), (1, 0)])]
    psum x1 -> x0, blocking collectives: 14.3 us -> none  [body(): total_sq = lax.psum(jnp.sum(gram_rows * gram_rows), 'ep')]
    dot_general x4 -> x7, matrix products: 17.8 us -> 7 us  [the longest x4 5.57 us: rows_dot_t(): lax.dot_general(rows, matrix, (((1,), (1,)), ((), ())), preferred_element...]
    scatter x2 -> x0, local copies, waits for them, and re-layouts: 8.51 us -> none  [body(): jnp.zeros((H, columns), jnp.bfloat16).at[target].set(incoming, mode='drop')]
  transfers between devices with their start and end apart: 4 -> 3, of which waited for: 4 -> 3; matrix products, arithmetic and copies ran while one was open for 2% -> 0% of each run, Pallas kernels for 0% -> 0%
where the time goes in v1:
time: 182 us
  blocking collectives  86.6 us (48%)
  waiting for transfers between devices  43.5 us (24%)
  starting transfers between devices  24.8 us (14%)
  between operations  14.9 us (8%)
  matrix products  7 us (4%)
  other arithmetic  3 us (2%)
  local copies, waits for them, and re-layouts  2.24 us (1%)
    all_to_all x7, blocking collectives, spread(): lax.all_to_all(jnp.broadcast_to(block[None], (size,) + block.shape), axis...  86.6 us
    all_gather x1, waiting for transfers between devices, body(): matrix = lax.all_gather(matrix, 'y', axis=0, tiled=True)  41.8 us
    ppermute x2, starting transfers between devices, swap(): return lax.ppermute(block, 'c', [(0, 1), (1, 0)])  24.8 us
    dot_general x4, matrix products, rows_dot_t(): lax.dot_general(rows, matrix, (((1,), (1,)), ((), ())), preferred_element...  5.57 us
  transfers between devices with their start and end apart: 3, of which 3 were waited for; matrix products, arithmetic and copies ran while one was open for 0% of the time, Pallas kernels for 0%

profile of v1, /device:TPU:1, one launch (start us, length us, event | category | flops | bytes accessed | tf_op | source)
XLA Modules:
  0.0 182.0 jit_solution(9049516819826042649)
XLA Ops:
  7.2 0.0 copy-start
  7.2 0.0 all-gather.2.cloned.1.call-start
  7.2 0.6 copy-done
  7.8 0.2 dynamic-slice_reduce_fusion
  8.0 1.5 fusion.6
  9.6 12.4 %collective-permute-start = (bf16[16,448]{1,0:T(8,128)(2,1)S(1)}, bf16[16,448]{1,0:T(8,128)(2,1)S(1)}, u32[]{:S(2)}, u32[]{:S(2)}) collective-permute-start(bf16[16,448]{1,0:T(8,128)(2,1)S(1)} %get-tuple-element.7), channel_id=1, source_target_pairs={{0,1},{1,0},{2,3},{3,2},{4,5},{5,4},{6,7},{7,6},{8,9},{9,8},{10,11... | collective-permute-start | bytes 43016 | tf_op jit(solution)/shard_map/ppermute | solution.py:29
  21.9 0.8 collective-permute-done
  22.8 0.1 pad_maximum_fusion
  22.9 22.9 %all_to_all.35 = bf16[12,16,896]{2,1,0:T(8,128)(2,1)} all-to-all(bf16[12,16,896]{2,1,0:T(8,128)(2,1)S(1)} %broadcast_in_dim.15), channel_id=1, replica_groups=mesh['z'=12,'y'=8,'x'=4,'c'=2] {'z'}, dimensions={0} | all-to-all | bytes 688128 | tf_op jit(solution)/shard_map/all_to_all | solution.py:23
  45.8 0.0 all-gather.2.cloned.1.call-update
  45.8 41.8 %all-gather.2.cloned.1.call-done = bf16[1536,896]{1,0:T(8,128)(2,1)} async-done(((bf16[192,896]{1,0:T(8,128)(2,1)}), bf16[1536,896]{1,0:T(8,128)(2,1)}) %all-gather.2.cloned.1.call-update) | async-done | bytes 2752528 | tf_op jit(solution)/shard_map/all_gather | solution.py:61
  87.7 0.0 copy-start.1
  87.7 2.7 %convolution_convert_fusion.3 = bf16[16,1536]{1,0:T(8,128)(2,1)S(1)} fusion(bf16[16,896]{1,0:T(8,128)(2,1)S(1)} %pad_maximum_fusion, bf16[1536,896]{1,0:T(8,128)(2,1)} %all-gather.2.cloned.1.call-done), kind=kOutput, calls=%fused_computation.3 | convolution fusion | flops 44064768 | bytes 2830336 | tf_op jit(solution)/shard_map/dot_general | solution.py:37
  90.4 8.9 %all_to_all.36 = bf16[4,16,1536]{2,1,0:T(8,128)(2,1)S(1)} all-to-all(bf16[4,16,1536]{2,1,0:T(8,128)(2,1)S(1)} %broadcast_in_dim.16), channel_id=1, replica_groups=mesh['z'=12,'y'=8,'x'=4,'c'=2] {'x'}, dimensions={0} | all-to-all | bytes 393216 | tf_op jit(solution)/shard_map/all_to_all | solution.py:23
  99.4 0.6 multiply_reduce_fusion
  100.0 0.6 broadcast_in_dim_broadcast_in_dim_broadcast_in_dim.3
  100.7 19.4 %all_to_all.37 = f32[12,8,128]{2,1,0:T(8,128)S(1)} all-to-all(f32[12,8,128]{2,1,0:T(8,128)S(1)} %broadcast_in_dim_broadcast_in_dim_broadcast_in_dim.3), channel_id=1, replica_groups=mesh['z'=12,'y'=8,'x'=4,'c'=2] {'z'}, dimensions={0} | all-to-all | bytes 98304 | tf_op jit(solution)/shard_map/all_to_all | solution.py:23
  120.1 11.3 %all_to_all.38 = f32[8,8,128]{2,1,0:T(8,128)S(1)} all-to-all(f32[8,8,128]{2,1,0:T(8,128)S(1)} %broadcast_in_dim.17), channel_id=1, replica_groups=mesh['z'=12,'y'=8,'x'=4,'c'=2] {'y'}, dimensions={0} | all-to-all | bytes 65536 | tf_op jit(solution)/shard_map/all_to_all | solution.py:23
  131.4 0.5 slice.19
  132.7 0.0 copy-done.1
  132.7 0.5 convolution_multiply_fusion.2
  133.2 0.8 convolution_convert_fusion.2
  134.1 7.5 %all_to_all.39 = bf16[4,16,1536]{2,1,0:T(8,128)(2,1)S(1)} all-to-all(bf16[4,16,1536]{2,1,0:T(8,128)(2,1)S(1)} %broadcast_in_dim.18), channel_id=1, replica_groups=mesh['z'=12,'y'=8,'x'=4,'c'=2] {'x'}, dimensions={0} | all-to-all | bytes 393216 | tf_op jit(solution)/shard_map/all_to_all | solution.py:23
  141.6 1.2 convolution_convert_fusion.1
  142.9 7.5 %all_to_all.40 = bf16[4,16,1536]{2,1,0:T(8,128)(2,1)S(1)} all-to-all(bf16[4,16,1536]{2,1,0:T(8,128)(2,1)S(1)} %broadcast_in_dim.19), channel_id=1, replica_groups=mesh['z'=12,'y'=8,'x'=4,'c'=2] {'x'}, dimensions={0} | all-to-all | bytes 393216 | tf_op jit(solution)/shard_map/all_to_all | solution.py:23
  150.4 0.5 convolution_convert_fusion.4
  150.9 0.8 convolution_convert_fusion
  151.8 8.9 %all_to_all.41 = bf16[4,16,1536]{2,1,0:T(8,128)(2,1)S(1)} all-to-all(bf16[4,16,1536]{2,1,0:T(8,128)(2,1)S(1)} %broadcast_in_dim.20), channel_id=1, replica_groups=mesh['z'=12,'y'=8,'x'=4,'c'=2] {'x'}, dimensions={0} | all-to-all | bytes 393216 | tf_op jit(solution)/shard_map/all_to_all | solution.py:23
  160.7 0.5 fusion.5
  161.2 0.1 slice.25
  161.2 12.4 %collective-permute-start.1 = (bf16[16,448]{1,0:T(8,128)(2,1)S(1)}, bf16[16,448]{1,0:T(8,128)(2,1)S(1)}, u32[]{:S(2)}, u32[]{:S(2)}) collective-permute-start(bf16[16,448]{1,0:T(8,128)(2,1)S(1)} %slice.25), channel_id=1, source_target_pairs={{0,1},{1,0},{2,3},{3,2},{4,5},{5,4},{6,7},{7,6},{8,9},{9,8},{10,11... | collective-permute-start | bytes 43016 | tf_op jit(solution)/shard_map/ppermute | solution.py:29
  173.6 0.8 collective-permute-done.1
  174.5 0.6 convert_multiply_fusion.2
  (14 shorter events, 0.3 us)
Async XLA Ops:
  7.2 0.7 copy-start
  7.2 80.5 %all-gather.2.cloned.1.call-start = ((), (), s32[]{:S(2)}) async-start(), calls=%async_computation.7 | async-start | bytes 3096576 | tf_op jit(solution)/shard_map/all_gather | solution.py:61
  9.6 13.2 %collective-permute-start = (bf16[16,448]{1,0:T(8,128)(2,1)S(1)}, bf16[16,448]{1,0:T(8,128)(2,1)S(1)}, u32[]{:S(2)}, u32[]{:S(2)}) collective-permute-start(bf16[16,448]{1,0:T(8,128)(2,1)S(1)} %get-tuple-element.7), channel_id=1, source_target_pairs={{0,1},{1,0},{2,3},{3,2},{4,5},{5,4},{6,7},{7,6},{8,9},{9,8},{10,11... | collective-permute-start | bytes 43016 | tf_op jit(solution)/shard_map/ppermute | solution.py:29
  87.7 45.0 %copy-start.1 = (bf16[1536,896]{1,0:T(8,128)(2,1)S(1)}, bf16[1536,896]{1,0:T(8,128)(2,1)}, u32[]{:S(2)}) copy-start(bf16[1536,896]{1,0:T(8,128)(2,1)} %all-gather.2.cloned.1.call-done) | copy-start | bytes 8257540
  161.2 13.2 %collective-permute-start.1 = (bf16[16,448]{1,0:T(8,128)(2,1)S(1)}, bf16[16,448]{1,0:T(8,128)(2,1)S(1)}, u32[]{:S(2)}, u32[]{:S(2)}) collective-permute-start(bf16[16,448]{1,0:T(8,128)(2,1)S(1)} %slice.25), channel_id=1, source_target_pairs={{0,1},{1,0},{2,3},{3,2},{4,5},{5,4},{6,7},{7,6},{8,9},{9,8},{10,11... | collective-permute-start | bytes 43016 | tf_op jit(solution)/shard_map/ppermute | solution.py:29
Sparse Core Ops, SparseCore 0:
  45.9 41.6 all-gather.1

commit v2 on v1

--- a/solution.py
+++ b/solution.py
@@ -57,13 +57,22 @@
     theirs = jnp.where(first_core, rounded[1], rounded[0])
     rows = jnp.concatenate([mine, swap(theirs)], axis=1)
     columns = rows.shape[1]
-    matrix = spread(rows, "z", NZ).reshape(-1, columns)
-    matrix = lax.all_gather(matrix, "y", axis=0, tiled=True)
+    same_y = spread(rows, "z", NZ).reshape(-1, columns)
+    matrix = lax.all_gather(same_y, "y", axis=0, tiled=True)
 
-    gram = sum_columns(rows_dot_t(rows, matrix))
-    total_sq = jnp.broadcast_to(jnp.sum(gram * gram), (8, 128))
-    total_sq = jnp.sum(spread(total_sq, "z", NZ), axis=0)
-    total_sq = jnp.sum(spread(total_sq, "y", NY), axis=0)[0, 0]
+    rows_later, same_y = lax.optimization_barrier((rows, same_y))
+    same_z = spread(rows_later, "y", NY).reshape(-1, columns)
+    block = sum_columns(rows_dot_t(same_z, same_y))
+    total_sq = jnp.broadcast_to(jnp.sum(block * block), (8, 128))
+    total_sq = jnp.sum(spread(total_sq, "z", NZ), axis=0)[0, 0]
+    block = block.reshape(NY, -1, block.shape[1])
+    held = block.shape[1]
+    block = jnp.concatenate(
+        [block, jnp.broadcast_to(total_sq, (NY, 8, block.shape[2]))], axis=1
+    )
+    block = lax.all_to_all(block, "y", 0, 0)
+    gram = jnp.concatenate([block[y, :held] for y in range(NY)], axis=1)
+    total_sq = jnp.sum(block[:, held:], axis=0)[0, 0]
     scale_sq = lax.rsqrt(total_sq + EPSILON)
     factor = jnp.sqrt(scale_sq)
 

time: 182 us -> 153 us (0.84)
  waiting for transfers between devices: 43.5 us -> 11.3 us
  starting transfers between devices: 24.8 us -> 29.9 us
  blocking collectives: 86.6 us -> 81.9 us
  local copies, waits for them, and re-layouts: 2.24 us -> 4.46 us
    all_gather x1, waiting for transfers between devices: 41.8 us -> 0.02 us  [body(): matrix = lax.all_gather(same_y, 'y', axis=0, tiled=True)]
    all_to_all x7 -> x6, blocking collectives: 86.6 us -> 70.8 us  [spread(): lax.all_to_all(jnp.broadcast_to(block[None], (size,) + block.shape), axis...]
    all_to_all x0 -> x1, blocking collectives: none -> 11 us  [body(): block = lax.all_to_all(block, 'y', 0, 0)]
    all_to_all x0 -> x1, waiting for transfers between devices: none -> 9.58 us  [spread(): lax.all_to_all(jnp.broadcast_to(block[None], (size,) + block.shape), axis...]
    all_to_all x0 -> x1, starting transfers between devices: none -> 5.29 us  [spread(): lax.all_to_all(jnp.broadcast_to(block[None], (size,) + block.shape), axis...]
    dot_general x3, matrix products: 1.43 us -> 3.35 us  [rows_dot(): jnp.dot(rows.astype(jnp.bfloat16), matrix, preferred_element_type=jnp.flo...]
  transfers between devices with their start and end apart: 3 -> 4, of which waited for: 3 -> 3; matrix products, arithmetic and copies ran while one was open for 0% -> 3% of each run, Pallas kernels for 0% -> 0%
where the time goes in v2:
time: 153 us
  blocking collectives  81.9 us (54%)
  starting transfers between devices  29.9 us (20%)
  between operations  14.9 us (10%)
  waiting for transfers between devices  11.3 us (7%)
  matrix products  7.41 us (5%)
  local copies, waits for them, and re-layouts  4.46 us (3%)
  other arithmetic  3.07 us (2%)
    all_to_all x6, blocking collectives, spread(): lax.all_to_all(jnp.broadcast_to(block[None], (size,) + block.shape), axis...  70.8 us
    ppermute x2, starting transfers between devices, swap(): return lax.ppermute(block, 'c', [(0, 1), (1, 0)])  24.6 us
    all_to_all x1, blocking collectives, body(): block = lax.all_to_all(block, 'y', 0, 0)  11 us
    all_to_all x1, waiting for transfers between devices, spread(): lax.all_to_all(jnp.broadcast_to(block[None], (size,) + block.shape), axis...  9.58 us
    all_to_all x1, starting transfers between devices, spread(): lax.all_to_all(jnp.broadcast_to(block[None], (size,) + block.shape), axis...  5.29 us
    dot_general x4, matrix products, rows_dot_t(): lax.dot_general(rows, matrix, (((1,), (1,)), ((), ())), preferred_element...  4.05 us
    dot_general x3, matrix products, rows_dot(): jnp.dot(rows.astype(jnp.bfloat16), matrix, preferred_element_type=jnp.flo...  3.35 us
  transfers between devices with their start and end apart: 4, of which 3 were waited for; matrix products, arithmetic and copies ran while one was open for 3% of the time, Pallas kernels for 0%

profile of v2, /device:TPU:1, one launch (start us, length us, event | category | flops | bytes accessed | tf_op | source)
XLA Modules:
  0.0 152.9 jit_solution(8615052696408721658)
XLA Ops:
  7.2 0.0 copy-start
  7.2 0.0 all-gather.2.cloned.1.call-start
  7.2 0.6 copy-done
  7.8 0.2 dynamic-slice_reduce_fusion
  8.0 1.5 fusion.6
  9.6 12.4 %collective-permute-start = (bf16[16,448]{1,0:T(8,128)(2,1)S(1)}, bf16[16,448]{1,0:T(8,128)(2,1)S(1)}, u32[]{:S(2)}, u32[]{:S(2)}) collective-permute-start(bf16[16,448]{1,0:T(8,128)(2,1)S(1)} %get-tuple-element.19), channel_id=1, source_target_pairs={{0,1},{1,0},{2,3},{3,2},{4,5},{5,4},{6,7},{7,6},{8,9},{9,8},{10,11... | collective-permute-start | bytes 43016 | tf_op jit(solution)/shard_map/ppermute | solution.py:29
  21.9 0.8 collective-permute-done
  22.8 0.1 pad_maximum_fusion
  22.9 22.9 %all_to_all.40 = bf16[12,16,896]{2,1,0:T(8,128)(2,1)} all-to-all(bf16[12,16,896]{2,1,0:T(8,128)(2,1)S(1)} %broadcast_in_dim.15), channel_id=1, replica_groups=mesh['z'=12,'y'=8,'x'=4,'c'=2] {'z'}, dimensions={0} | all-to-all | bytes 688128 | tf_op jit(solution)/shard_map/all_to_all | solution.py:23
  45.8 0.0 all-gather.2.cloned.1.call-update
  45.9 15.6 %all_to_all.41 = bf16[8,16,896]{2,1,0:T(8,128)(2,1)S(1)} all-to-all(bf16[8,16,896]{2,1,0:T(8,128)(2,1)S(1)} %broadcast_in_dim.16), channel_id=1, replica_groups=mesh['z'=12,'y'=8,'x'=4,'c'=2] {'y'}, dimensions={0} | all-to-all | bytes 458752 | tf_op jit(solution)/shard_map/all_to_all | solution.py:23
  61.5 1.2 convolution_convert_fusion.3
  62.8 9.1 %all_to_all.42 = bf16[4,128,192]{1,2,0:T(8,128)(2,1)S(1)} all-to-all(bf16[4,128,192]{1,2,0:T(8,128)(2,1)S(1)} %broadcast_in_dim.17), channel_id=1, replica_groups=mesh['z'=12,'y'=8,'x'=4,'c'=2] {'x'}, dimensions={0} | all-to-all | bytes 393216 | tf_op jit(solution)/shard_map/all_to_all | solution.py:23
  71.9 0.7 multiply_reduce_fusion
  72.6 1.3 broadcast_in_dim_broadcast_in_dim_broadcast_in_dim.3
  73.9 5.3 %all-to-all-start.3 = ((f32[12,8,128]{2,1,0:T(8,128)}), f32[12,8,128]{2,1,0:T(8,128)S(1)}, u32[]{:S(2)}, u32[]{:S(2)}) async-start(f32[12,8,128]{2,1,0:T(8,128)} %broadcast_in_dim_broadcast_in_dim_broadcast_in_dim.3), calls=%async_computation.3 | async-start | bytes 98304 | tf_op jit(solution)/shard_map/all_to_all | solution.py:23
  79.2 0.1 copy.14
  79.3 9.6 %all-to-all-done.3 = f32[12,8,128]{2,1,0:T(8,128)S(1)} async-done(((f32[12,8,128]{2,1,0:T(8,128)}), f32[12,8,128]{2,1,0:T(8,128)S(1)}, u32[]{:S(2)}, u32[]{:S(2)}) %all-to-all-start.3) | async-done | bytes 49184 | tf_op jit(solution)/shard_map/all_to_all | solution.py:23
  88.9 0.5 slice.49
  89.4 0.7 concatenate.10
  90.0 11.0 %all_to_all.43 = f32[8,24,192]{2,1,0:T(8,128)S(1)} all-to-all(f32[8,24,192]{2,1,0:T(8,128)S(1)} %concatenate.10), channel_id=1, replica_groups=mesh['z'=12,'y'=8,'x'=4,'c'=2] {'y'}, dimensions={0} | all-to-all | bytes 294912 | tf_op jit(solution)/shard_map/all_to_all | solution.py:73
  101.1 0.5 slice.65
  102.3 0.1 concatenate.11
  102.4 0.0 all-gather.2.cloned.1.call-done
  102.5 0.0 copy-start.1
  102.5 2.4 %convolution_multiply_fusion.2 = f32[16,896]{1,0:T(8,128)S(1)} fusion(bf16[1536,896]{1,0:T(8,128)(2,1)} %all-gather.2.cloned.1.call-done, f32[16,1536]{1,0:T(8,128)S(1)} %concatenate.11, f32[]{:T(128)} %bitcast.6), kind=kOutput, calls=%fused_computation.10 | convolution fusion | flops 44103680 | bytes 2908164 | tf_op jit(solution)/shard_map/dot_general | solution.py:43
  104.9 0.2 copy-done.1
  105.1 0.8 convolution_convert_fusion.2
  105.9 7.5 %all_to_all.44 = bf16[4,16,1536]{2,1,0:T(8,128)(2,1)S(1)} all-to-all(bf16[4,16,1536]{2,1,0:T(8,128)(2,1)S(1)} %broadcast_in_dim.18), channel_id=1, replica_groups=mesh['z'=12,'y'=8,'x'=4,'c'=2] {'x'}, dimensions={0} | all-to-all | bytes 393216 | tf_op jit(solution)/shard_map/all_to_all | solution.py:23
  113.5 1.2 convolution_convert_fusion.1
  114.7 7.5 %all_to_all.45 = bf16[4,16,1536]{2,1,0:T(8,128)(2,1)S(1)} all-to-all(bf16[4,16,1536]{2,1,0:T(8,128)(2,1)S(1)} %broadcast_in_dim.19), channel_id=1, replica_groups=mesh['z'=12,'y'=8,'x'=4,'c'=2] {'x'}, dimensions={0} | all-to-all | bytes 393216 | tf_op jit(solution)/shard_map/all_to_all | solution.py:23
  122.3 0.5 convolution_convert_fusion.4
  122.8 0.8 convolution_convert_fusion
  123.6 8.1 %all_to_all.46 = bf16[4,16,1536]{2,1,0:T(8,128)(2,1)S(1)} all-to-all(bf16[4,16,1536]{2,1,0:T(8,128)(2,1)S(1)} %broadcast_in_dim.20), channel_id=1, replica_groups=mesh['z'=12,'y'=8,'x'=4,'c'=2] {'x'}, dimensions={0} | all-to-all | bytes 393216 | tf_op jit(solution)/shard_map/all_to_all | solution.py:23
  131.8 0.5 fusion.5
  132.3 0.1 slice.75
  132.4 12.2 %collective-permute-start.1 = (bf16[16,448]{1,0:T(8,128)(2,1)S(1)}, bf16[16,448]{1,0:T(8,128)(2,1)S(1)}, u32[]{:S(2)}, u32[]{:S(2)}) collective-permute-start(bf16[16,448]{1,0:T(8,128)(2,1)S(1)} %slice.75), channel_id=1, source_target_pairs={{0,1},{1,0},{2,3},{3,2},{4,5},{5,4},{6,7},{7,6},{8,9},{9,8},{10,11... | collective-permute-start | bytes 43016 | tf_op jit(solution)/shard_map/ppermute | solution.py:29
  144.6 0.8 collective-permute-done.1
  145.4 0.6 convert_multiply_fusion.2
  (15 shorter events, 0.3 us)
Async XLA Ops:
  7.2 0.7 copy-start
  7.2 95.3 %all-gather.2.cloned.1.call-start = ((), (), s32[]{:S(2)}) async-start(), calls=%async_computation.8 | async-start | bytes 3096576 | tf_op jit(solution)/shard_map/all_gather | solution.py:61
  9.6 13.2 %collective-permute-start = (bf16[16,448]{1,0:T(8,128)(2,1)S(1)}, bf16[16,448]{1,0:T(8,128)(2,1)S(1)}, u32[]{:S(2)}, u32[]{:S(2)}) collective-permute-start(bf16[16,448]{1,0:T(8,128)(2,1)S(1)} %get-tuple-element.19), channel_id=1, source_target_pairs={{0,1},{1,0},{2,3},{3,2},{4,5},{5,4},{6,7},{7,6},{8,9},{9,8},{10,11... | collective-permute-start | bytes 43016 | tf_op jit(solution)/shard_map/ppermute | solution.py:29
  73.9 15.0 %all-to-all-start.3 = ((f32[12,8,128]{2,1,0:T(8,128)}), f32[12,8,128]{2,1,0:T(8,128)S(1)}, u32[]{:S(2)}, u32[]{:S(2)}) async-start(f32[12,8,128]{2,1,0:T(8,128)} %broadcast_in_dim_broadcast_in_dim_broadcast_in_dim.3), calls=%async_computation.3 | async-start | bytes 98304 | tf_op jit(solution)/shard_map/all_to_all | solution.py:23
  102.5 2.6 %copy-start.1 = (bf16[1536,896]{1,0:T(8,128)(2,1)S(1)}, bf16[1536,896]{1,0:T(8,128)(2,1)}, u32[]{:S(2)}) copy-start(bf16[1536,896]{1,0:T(8,128)(2,1)} %all-gather.2.cloned.1.call-done) | copy-start | bytes 8257540
  132.4 13.0 %collective-permute-start.1 = (bf16[16,448]{1,0:T(8,128)(2,1)S(1)}, bf16[16,448]{1,0:T(8,128)(2,1)S(1)}, u32[]{:S(2)}, u32[]{:S(2)}) collective-permute-start(bf16[16,448]{1,0:T(8,128)(2,1)S(1)} %slice.75), channel_id=1, source_target_pairs={{0,1},{1,0},{2,3},{3,2},{4,5},{5,4},{6,7},{7,6},{8,9},{9,8},{10,11... | collective-permute-start | bytes 43016 | tf_op jit(solution)/shard_map/ppermute | solution.py:29
Sparse Core Ops, SparseCore 0:
  45.9 42.2 all-gather.1

commit v3 on v2

--- a/solution.py
+++ b/solution.py
@@ -57,11 +57,11 @@
     theirs = jnp.where(first_core, rounded[1], rounded[0])
     rows = jnp.concatenate([mine, swap(theirs)], axis=1)
     columns = rows.shape[1]
-    same_y = spread(rows, "z", NZ).reshape(-1, columns)
+    same_z = spread(rows, "y", NY).reshape(-1, columns)
+    rows_later, same_z = lax.optimization_barrier((rows, same_z))
+    same_y = spread(rows_later, "z", NZ).reshape(-1, columns)
     matrix = lax.all_gather(same_y, "y", axis=0, tiled=True)
 
-    rows_later, same_y = lax.optimization_barrier((rows, same_y))
-    same_z = spread(rows_later, "y", NY).reshape(-1, columns)
     block = sum_columns(rows_dot_t(same_z, same_y))
     total_sq = jnp.broadcast_to(jnp.sum(block * block), (8, 128))
     total_sq = jnp.sum(spread(total_sq, "z", NZ), axis=0)[0, 0]

time: 153 us -> 153 us (level)
  starting transfers between devices: 29.9 us -> 27.9 us
  blocking collectives: 81.9 us -> 83.6 us
    ppermute x2, starting transfers between devices: 24.6 us -> 21.8 us  [swap(): return lax.ppermute(block, 'c', [(0, 1), (1, 0)])]
    all_to_all x1, blocking collectives: 11 us -> 13.5 us  [body(): block = lax.all_to_all(block, 'y', 0, 0)]
where the time goes in v3:
time: 153 us
  blocking collectives  83.6 us (55%)
  starting transfers between devices  27.9 us (18%)
  between operations  14.9 us (10%)
  waiting for transfers between devices  11.3 us (7%)
  matrix products  7.41 us (5%)
  local copies, waits for them, and re-layouts  4.46 us (3%)
  other arithmetic  3.07 us (2%)
    all_to_all x6, blocking collectives, spread(): lax.all_to_all(jnp.broadcast_to(block[None], (size,) + block.shape), axis...  70.1 us
    ppermute x2, starting transfers between devices, swap(): return lax.ppermute(block, 'c', [(0, 1), (1, 0)])  21.8 us
    all_to_all x1, blocking collectives, body(): block = lax.all_to_all(block, 'y', 0, 0)  13.5 us
    all_to_all x1, waiting for transfers between devices, spread(): lax.all_to_all(jnp.broadcast_to(block[None], (size,) + block.shape), axis...  9.58 us
    all_to_all x1, starting transfers between devices, spread(): lax.all_to_all(jnp.broadcast_to(block[None], (size,) + block.shape), axis...  6.04 us
    dot_general x4, matrix products, rows_dot_t(): lax.dot_general(rows, matrix, (((1,), (1,)), ((), ())), preferred_element...  4.06 us
    dot_general x3, matrix products, rows_dot(): jnp.dot(rows.astype(jnp.bfloat16), matrix, preferred_element_type=jnp.flo...  3.35 us
  transfers between devices with their start and end apart: 4, of which 3 were waited for; matrix products, arithmetic and copies ran while one was open for 3% of the time, Pallas kernels for 0%

profile of v3, /device:TPU:1, one launch (start us, length us, event | category | flops | bytes accessed | tf_op | source)
XLA Modules:
  0.0 152.7 jit_solution(267224928886938570)
XLA Ops:
  7.2 0.0 copy-start
  7.2 0.0 all-gather.2.cloned.1.call-start
  7.2 0.6 copy-done
  7.8 0.2 dynamic-slice_reduce_fusion
  8.0 1.5 fusion.6
  9.6 12.4 %collective-permute-start = (bf16[16,448]{1,0:T(8,128)(2,1)S(1)}, bf16[16,448]{1,0:T(8,128)(2,1)S(1)}, u32[]{:S(2)}, u32[]{:S(2)}) collective-permute-start(bf16[16,448]{1,0:T(8,128)(2,1)S(1)} %get-tuple-element.19), channel_id=1, source_target_pairs={{0,1},{1,0},{2,3},{3,2},{4,5},{5,4},{6,7},{7,6},{8,9},{9,8},{10,11... | collective-permute-start | bytes 43016 | tf_op jit(solution)/shard_map/ppermute | solution.py:29
  21.9 0.8 collective-permute-done
  22.8 0.1 pad_maximum_fusion
  22.9 14.0 %all_to_all.40 = bf16[8,16,896]{2,1,0:T(8,128)(2,1)S(1)} all-to-all(bf16[8,16,896]{2,1,0:T(8,128)(2,1)S(1)} %broadcast_in_dim.15), channel_id=1, replica_groups=mesh['z'=12,'y'=8,'x'=4,'c'=2] {'y'}, dimensions={0} | all-to-all | bytes 458752 | tf_op jit(solution)/shard_map/all_to_all | solution.py:23
  36.9 23.8 %all_to_all.41 = bf16[12,16,896]{2,1,0:T(8,128)(2,1)} all-to-all(bf16[12,16,896]{2,1,0:T(8,128)(2,1)S(1)} %broadcast_in_dim.16), channel_id=1, replica_groups=mesh['z'=12,'y'=8,'x'=4,'c'=2] {'z'}, dimensions={0} | all-to-all | bytes 688128 | tf_op jit(solution)/shard_map/all_to_all | solution.py:23
  60.6 0.0 all-gather.2.cloned.1.call-update
  60.7 1.2 convolution_convert_fusion.3
  62.0 9.0 %all_to_all.42 = bf16[4,128,192]{1,2,0:T(8,128)(2,1)S(1)} all-to-all(bf16[4,128,192]{1,2,0:T(8,128)(2,1)S(1)} %broadcast_in_dim.17), channel_id=1, replica_groups=mesh['z'=12,'y'=8,'x'=4,'c'=2] {'x'}, dimensions={0} | all-to-all | bytes 393216 | tf_op jit(solution)/shard_map/all_to_all | solution.py:23
  71.0 0.7 multiply_reduce_fusion
  71.7 1.3 broadcast_in_dim_broadcast_in_dim_broadcast_in_dim.3
  73.0 6.0 %all-to-all-start.3 = ((f32[12,8,128]{2,1,0:T(8,128)}), f32[12,8,128]{2,1,0:T(8,128)S(1)}, u32[]{:S(2)}, u32[]{:S(2)}) async-start(f32[12,8,128]{2,1,0:T(8,128)} %broadcast_in_dim_broadcast_in_dim_broadcast_in_dim.3), calls=%async_computation.3 | async-start | bytes 98304 | tf_op jit(solution)/shard_map/all_to_all | solution.py:23
  79.0 0.1 copy.14
  79.1 9.6 %all-to-all-done.3 = f32[12,8,128]{2,1,0:T(8,128)S(1)} async-done(((f32[12,8,128]{2,1,0:T(8,128)}), f32[12,8,128]{2,1,0:T(8,128)S(1)}, u32[]{:S(2)}, u32[]{:S(2)}) %all-to-all-start.3) | async-done | bytes 49184 | tf_op jit(solution)/shard_map/all_to_all | solution.py:23
  88.7 0.5 slice.49
  89.2 0.7 concatenate.10
  89.9 13.5 %all_to_all.43 = f32[8,24,192]{2,1,0:T(8,128)S(1)} all-to-all(f32[8,24,192]{2,1,0:T(8,128)S(1)} %concatenate.10), channel_id=1, replica_groups=mesh['z'=12,'y'=8,'x'=4,'c'=2] {'y'}, dimensions={0} | all-to-all | bytes 294912 | tf_op jit(solution)/shard_map/all_to_all | solution.py:73
  103.5 0.5 slice.65
  104.7 0.1 concatenate.11
  104.8 0.0 all-gather.2.cloned.1.call-done
  104.9 0.0 copy-start.1
  104.9 2.4 %convolution_multiply_fusion.2 = f32[16,896]{1,0:T(8,128)S(1)} fusion(bf16[1536,896]{1,0:T(8,128)(2,1)} %all-gather.2.cloned.1.call-done, f32[16,1536]{1,0:T(8,128)S(1)} %concatenate.11, f32[]{:T(128)} %bitcast.6), kind=kOutput, calls=%fused_computation.10 | convolution fusion | flops 44103680 | bytes 2908164 | tf_op jit(solution)/shard_map/dot_general | solution.py:43
  107.3 0.2 copy-done.1
  107.5 0.8 convolution_convert_fusion.2
  108.3 8.3 %all_to_all.44 = bf16[4,16,1536]{2,1,0:T(8,128)(2,1)S(1)} all-to-all(bf16[4,16,1536]{2,1,0:T(8,128)(2,1)S(1)} %broadcast_in_dim.18), channel_id=1, replica_groups=mesh['z'=12,'y'=8,'x'=4,'c'=2] {'x'}, dimensions={0} | all-to-all | bytes 393216 | tf_op jit(solution)/shard_map/all_to_all | solution.py:23
  116.6 1.2 convolution_convert_fusion.1
  117.8 7.5 %all_to_all.45 = bf16[4,16,1536]{2,1,0:T(8,128)(2,1)S(1)} all-to-all(bf16[4,16,1536]{2,1,0:T(8,128)(2,1)S(1)} %broadcast_in_dim.19), channel_id=1, replica_groups=mesh['z'=12,'y'=8,'x'=4,'c'=2] {'x'}, dimensions={0} | all-to-all | bytes 393216 | tf_op jit(solution)/shard_map/all_to_all | solution.py:23
  125.4 0.5 convolution_convert_fusion.4
  125.9 0.8 convolution_convert_fusion
  126.8 7.5 %all_to_all.46 = bf16[4,16,1536]{2,1,0:T(8,128)(2,1)S(1)} all-to-all(bf16[4,16,1536]{2,1,0:T(8,128)(2,1)S(1)} %broadcast_in_dim.20), channel_id=1, replica_groups=mesh['z'=12,'y'=8,'x'=4,'c'=2] {'x'}, dimensions={0} | all-to-all | bytes 393216 | tf_op jit(solution)/shard_map/all_to_all | solution.py:23
  134.3 0.5 fusion.5
  134.8 0.1 slice.75
  134.9 9.5 %collective-permute-start.1 = (bf16[16,448]{1,0:T(8,128)(2,1)S(1)}, bf16[16,448]{1,0:T(8,128)(2,1)S(1)}, u32[]{:S(2)}, u32[]{:S(2)}) collective-permute-start(bf16[16,448]{1,0:T(8,128)(2,1)S(1)} %slice.75), channel_id=1, source_target_pairs={{0,1},{1,0},{2,3},{3,2},{4,5},{5,4},{6,7},{7,6},{8,9},{9,8},{10,11... | collective-permute-start | bytes 43016 | tf_op jit(solution)/shard_map/ppermute | solution.py:29
  144.4 0.8 collective-permute-done.1
  145.2 0.6 convert_multiply_fusion.2
  (15 shorter events, 0.3 us)
Async XLA Ops:
  7.2 0.7 copy-start
  7.2 97.7 %all-gather.2.cloned.1.call-start = ((), (), s32[]{:S(2)}) async-start(), calls=%async_computation.8 | async-start | bytes 3096576 | tf_op jit(solution)/shard_map/all_gather | solution.py:63
  9.6 13.2 %collective-permute-start = (bf16[16,448]{1,0:T(8,128)(2,1)S(1)}, bf16[16,448]{1,0:T(8,128)(2,1)S(1)}, u32[]{:S(2)}, u32[]{:S(2)}) collective-permute-start(bf16[16,448]{1,0:T(8,128)(2,1)S(1)} %get-tuple-element.19), channel_id=1, source_target_pairs={{0,1},{1,0},{2,3},{3,2},{4,5},{5,4},{6,7},{7,6},{8,9},{9,8},{10,11... | collective-permute-start | bytes 43016 | tf_op jit(solution)/shard_map/ppermute | solution.py:29
  73.0 15.7 %all-to-all-start.3 = ((f32[12,8,128]{2,1,0:T(8,128)}), f32[12,8,128]{2,1,0:T(8,128)S(1)}, u32[]{:S(2)}, u32[]{:S(2)}) async-start(f32[12,8,128]{2,1,0:T(8,128)} %broadcast_in_dim_broadcast_in_dim_broadcast_in_dim.3), calls=%async_computation.3 | async-start | bytes 98304 | tf_op jit(solution)/shard_map/all_to_all | solution.py:23
  104.9 2.6 %copy-start.1 = (bf16[1536,896]{1,0:T(8,128)(2,1)S(1)}, bf16[1536,896]{1,0:T(8,128)(2,1)}, u32[]{:S(2)}) copy-start(bf16[1536,896]{1,0:T(8,128)(2,1)} %all-gather.2.cloned.1.call-done) | copy-start | bytes 8257540
  134.9 10.3 %collective-permute-start.1 = (bf16[16,448]{1,0:T(8,128)(2,1)S(1)}, bf16[16,448]{1,0:T(8,128)(2,1)S(1)}, u32[]{:S(2)}, u32[]{:S(2)}) collective-permute-start(bf16[16,448]{1,0:T(8,128)(2,1)S(1)} %slice.75), channel_id=1, source_target_pairs={{0,1},{1,0},{2,3},{3,2},{4,5},{5,4},{6,7},{7,6},{8,9},{9,8},{10,11... | collective-permute-start | bytes 43016 | tf_op jit(solution)/shard_map/ppermute | solution.py:29
Sparse Core Ops, SparseCore 0:
  60.8 42.0 all-gather.1

commit v4 on v2

--- a/solution.py
+++ b/solution.py
@@ -17,6 +17,16 @@
 SECOND_CUBE = -0.5
 
 NZ, NY, NX, NC = 12, 8, 4, 2
+PACKED = 256
+
+
+def three_parts(value):
+    parts = []
+    for _ in range(3):
+        part = lax.reduce_precision(value, 8, 7)
+        parts.append(part)
+        value = value - part
+    return parts
 
 
 def spread(block, axis, size):
@@ -63,21 +73,24 @@
     rows_later, same_y = lax.optimization_barrier((rows, same_y))
     same_z = spread(rows_later, "y", NY).reshape(-1, columns)
     block = sum_columns(rows_dot_t(same_z, same_y))
-    total_sq = jnp.broadcast_to(jnp.sum(block * block), (8, 128))
-    total_sq = jnp.sum(spread(total_sq, "z", NZ), axis=0)[0, 0]
-    block = block.reshape(NY, -1, block.shape[1])
-    held = block.shape[1]
-    block = jnp.concatenate(
-        [block, jnp.broadcast_to(total_sq, (NY, 8, block.shape[2]))], axis=1
-    )
+    total_sq = jnp.broadcast_to(jnp.sum(block * block, keepdims=True), (1, 128))
+    total_sq = jnp.sum(spread(total_sq, "z", NZ), axis=0)
+    block = block.astype(bf16).reshape(NY, -1, block.shape[1])
+    held = block.shape[2]
+    shape = block.shape[:2] + (PACKED - held,)
+    lane = lax.broadcasted_iota(jnp.int32, shape, 2)
+    packed = jnp.zeros(shape, f32)
+    for k, part in enumerate(three_parts(total_sq[:, : shape[2]])):
+        packed = jnp.where(lane == k, part[None], packed)
+    block = jnp.concatenate([block, packed.astype(bf16)], axis=2)
     block = lax.all_to_all(block, "y", 0, 0)
-    gram = jnp.concatenate([block[y, :held] for y in range(NY)], axis=1)
-    total_sq = jnp.sum(block[:, held:], axis=0)[0, 0]
+    gram = jnp.concatenate([block[y, :, :held] for y in range(NY)], axis=1)
+    total_sq = jnp.sum(block[:, :1, held:].astype(f32))
     scale_sq = lax.rsqrt(total_sq + EPSILON)
     factor = jnp.sqrt(scale_sq)
 
     first = (
-        factor * (FIRST_LIN * rows.astype(f32) + FIRST_CUBE * rows_dot(scale_sq * gram, matrix))
+        factor * (FIRST_LIN * rows.astype(f32) + FIRST_CUBE * (scale_sq * rows_dot(gram, matrix)))
     ).astype(bf16)
     product = rows_dot(scale_sq * sum_columns(rows_dot_t(first, matrix)), matrix)
     applied = (FIRST_LIN * first.astype(f32) + FIRST_CUBE * product).astype(bf16)

time: 153 us -> 151 us (0.987)
  blocking collectives: 81.9 us -> 71.4 us
  waiting for transfers between devices: 11.3 us -> 15.6 us
  starting transfers between devices: 29.9 us -> 33.9 us
    all_to_all x6 -> x5, blocking collectives: 70.8 us -> 61.8 us  [spread(): lax.all_to_all(jnp.broadcast_to(block[None], (size,) + block.shape), axis...]
    all_to_all x1 -> x2, waiting for transfers between devices: 9.58 us -> 14 us  [spread(): lax.all_to_all(jnp.broadcast_to(block[None], (size,) + block.shape), axis...]
    all_to_all x1 -> x2, starting transfers between devices: 5.29 us -> 9.32 us  [spread(): lax.all_to_all(jnp.broadcast_to(block[None], (size,) + block.shape), axis...]
  transfers between devices with their start and end apart: 4 -> 5, of which waited for: 3 -> 4; matrix products, arithmetic and copies ran while one was open for 3% -> 3% of each run, Pallas kernels for 0% -> 0%
where the time goes in v4:
time: 151 us
  blocking collectives  71.4 us (47%)
  starting transfers between devices  33.9 us (22%)
  waiting for transfers between devices  15.6 us (10%)
  between operations  14.9 us (10%)
  matrix products  7.41 us (5%)
  other arithmetic  3.88 us (3%)
  local copies, waits for them, and re-layouts  3.43 us (2%)
    all_to_all x5, blocking collectives, spread(): lax.all_to_all(jnp.broadcast_to(block[None], (size,) + block.shape), axis...  61.8 us
    ppermute x2, starting transfers between devices, swap(): return lax.ppermute(block, 'c', [(0, 1), (1, 0)])  24.6 us
    all_to_all x2, waiting for transfers between devices, spread(): lax.all_to_all(jnp.broadcast_to(block[None], (size,) + block.shape), axis...  14 us
    all_to_all x1, blocking collectives, body(): block = lax.all_to_all(block, 'y', 0, 0)  9.61 us
    all_to_all x2, starting transfers between devices, spread(): lax.all_to_all(jnp.broadcast_to(block[None], (size,) + block.shape), axis...  9.32 us
    dot_general x4, matrix products, rows_dot_t(): lax.dot_general(rows, matrix, (((1,), (1,)), ((), ())), preferred_element...  4.05 us
    dot_general x3, matrix products, rows_dot(): jnp.dot(rows.astype(jnp.bfloat16), matrix, preferred_element_type=jnp.flo...  3.35 us
  transfers between devices with their start and end apart: 5, of which 4 were waited for; matrix products, arithmetic and copies ran while one was open for 3% of the time, Pallas kernels for 0%

profile of v4, /device:TPU:1, one launch (start us, length us, event | category | flops | bytes accessed | tf_op | source)
XLA Modules:
  0.0 150.6 jit_solution(15002422872762698792)
XLA Ops:
  7.2 0.0 copy-start
  7.2 0.0 all-gather.2.cloned.1.call-start
  7.2 0.6 copy-done
  7.8 0.2 dynamic-slice_reduce_fusion
  8.0 1.5 %fusion.7 = (bf16[2,16,448]{2,1,0:T(8,128)(2,1)S(1)}, f32[2,16,448]{2,1,0:T(8,128)}) fusion(f32[2,16,448]{2,1,0:T(8,128)} %param.3, s32[2]{0:T(128)S(1)} %dynamic-slice_reduce_fusion, f32[2,16,448]{2,1,0:T(8,128)} %param.4), kind=kLoop, calls=%fused_computation.31 | loop fusion | flops 100352 | bytes 200712 | tf_op jit(solution)/shard_map/jit(_where)/select_n | solution.py:64
  9.6 12.4 %collective-permute-start = (bf16[16,448]{1,0:T(8,128)(2,1)S(1)}, bf16[16,448]{1,0:T(8,128)(2,1)S(1)}, u32[]{:S(2)}, u32[]{:S(2)}) collective-permute-start(bf16[16,448]{1,0:T(8,128)(2,1)S(1)} %get-tuple-element.21), channel_id=1, source_target_pairs={{0,1},{1,0},{2,3},{3,2},{4,5},{5,4},{6,7},{7,6},{8,9},{9,8},{10,11... | collective-permute-start | bytes 43016 | tf_op jit(solution)/shard_map/ppermute | solution.py:39
  21.9 0.8 collective-permute-done
  22.8 0.1 pad_maximum_fusion.1
  22.9 22.9 %all_to_all.40 = bf16[12,16,896]{2,1,0:T(8,128)(2,1)} all-to-all(bf16[12,16,896]{2,1,0:T(8,128)(2,1)S(1)} %broadcast_in_dim.72), channel_id=1, replica_groups=mesh['z'=12,'y'=8,'x'=4,'c'=2] {'z'}, dimensions={0} | all-to-all | bytes 688128 | tf_op jit(solution)/shard_map/all_to_all | solution.py:33
  45.8 0.0 all-gather.2.cloned.1.call-update
  45.9 15.6 %all_to_all.41 = bf16[8,16,896]{2,1,0:T(8,128)(2,1)S(1)} all-to-all(bf16[8,16,896]{2,1,0:T(8,128)(2,1)S(1)} %broadcast_in_dim.73), channel_id=1, replica_groups=mesh['z'=12,'y'=8,'x'=4,'c'=2] {'y'}, dimensions={0} | all-to-all | bytes 458752 | tf_op jit(solution)/shard_map/all_to_all | solution.py:33
  61.5 1.2 convolution_convert_fusion.3
  62.7 0.7 broadcast_in_dim.74
  63.4 4.0 %all-to-all-start.2 = ((bf16[4,128,192]{1,2,0:T(8,128)(2,1)}), bf16[4,128,192]{1,2,0:T(8,128)(2,1)S(1)}, u32[]{:S(2)}, u32[]{:S(2)}) async-start(bf16[4,128,192]{1,2,0:T(8,128)(2,1)} %broadcast_in_dim.74), calls=%async_computation.2 | async-start | bytes 393216 | tf_op jit(solution)/shard_map/all_to_all | solution.py:33
  67.5 5.2 %all-to-all-done.2 = bf16[4,128,192]{1,2,0:T(8,128)(2,1)S(1)} async-done(((bf16[4,128,192]{1,2,0:T(8,128)(2,1)}), bf16[4,128,192]{1,2,0:T(8,128)(2,1)S(1)}, u32[]{:S(2)}, u32[]{:S(2)}) %all-to-all-start.2) | async-done | bytes 196640 | tf_op jit(solution)/shard_map/all_to_all | solution.py:33
  72.7 0.7 fusion.23
  73.4 1.3 broadcast_in_dim_broadcast_in_dim_broadcast_in_dim.2
  74.7 5.3 %all-to-all-start.3 = ((f32[12,1,128]{2,1,0:T(1,128)}), f32[12,1,128]{2,1,0:T(1,128)S(1)}, u32[]{:S(2)}, u32[]{:S(2)}) async-start(f32[12,1,128]{2,1,0:T(1,128)} %broadcast_in_dim_broadcast_in_dim_broadcast_in_dim.2), calls=%async_computation.3 | async-start | bytes 12288 | tf_op jit(solution)/shard_map/all_to_all | solution.py:33
  80.0 0.1 copy.14
  80.1 8.7 %all-to-all-done.3 = f32[12,1,128]{2,1,0:T(1,128)S(1)} async-done(((f32[12,1,128]{2,1,0:T(1,128)}), f32[12,1,128]{2,1,0:T(1,128)S(1)}, u32[]{:S(2)}, u32[]{:S(2)}) %all-to-all-start.3) | async-done | bytes 6176 | tf_op jit(solution)/shard_map/all_to_all | solution.py:33
  88.9 0.1 pad_maximum_fusion
  89.0 9.6 %all_to_all.42 = bf16[8,16,256]{2,1,0:T(8,128)(2,1)S(1)} all-to-all(bf16[8,16,256]{2,1,0:T(8,128)(2,1)S(1)} %pad_maximum_fusion), channel_id=1, replica_groups=mesh['z'=12,'y'=8,'x'=4,'c'=2] {'y'}, dimensions={0} | all-to-all | bytes 131072 | tf_op jit(solution)/shard_map/all_to_all | solution.py:86
  98.6 0.7 fusion.17
  100.1 0.1 concatenate.11
  100.2 0.0 all-gather.2.cloned.1.call-done
  100.2 0.0 copy-start.1
  100.2 2.4 %fusion.4 = f32[16,896]{1,0:T(8,128)S(1)} fusion(bf16[16,1536]{1,0:T(8,128)(2,1)S(1)} %concatenate.11, bf16[1536,896]{1,0:T(8,128)(2,1)} %all-gather.2.cloned.1.call-done, f32[]{:T(128)S(6)} %rsqrt.3), kind=kOutput, calls=%fused_computation.11 | convolution fusion | flops 44068864 | bytes 2859012 | tf_op jit(solution)/shard_map/dot_general | solution.py:53
  102.6 0.2 copy-done.1
  102.8 0.8 convolution_convert_fusion.2
  103.6 7.5 %all_to_all.43 = bf16[4,16,1536]{2,1,0:T(8,128)(2,1)S(1)} all-to-all(bf16[4,16,1536]{2,1,0:T(8,128)(2,1)S(1)} %broadcast_in_dim.82), channel_id=1, replica_groups=mesh['z'=12,'y'=8,'x'=4,'c'=2] {'x'}, dimensions={0} | all-to-all | bytes 393216 | tf_op jit(solution)/shard_map/all_to_all | solution.py:33
  111.2 1.2 convolution_convert_fusion.1
  112.4 7.5 %all_to_all.44 = bf16[4,16,1536]{2,1,0:T(8,128)(2,1)S(1)} all-to-all(bf16[4,16,1536]{2,1,0:T(8,128)(2,1)S(1)} %broadcast_in_dim.83), channel_id=1, replica_groups=mesh['z'=12,'y'=8,'x'=4,'c'=2] {'x'}, dimensions={0} | all-to-all | bytes 393216 | tf_op jit(solution)/shard_map/all_to_all | solution.py:33
  120.0 0.5 convolution_convert_fusion.4
  120.5 0.8 convolution_convert_fusion
  121.4 8.1 %all_to_all.45 = bf16[4,16,1536]{2,1,0:T(8,128)(2,1)S(1)} all-to-all(bf16[4,16,1536]{2,1,0:T(8,128)(2,1)S(1)} %broadcast_in_dim.84), channel_id=1, replica_groups=mesh['z'=12,'y'=8,'x'=4,'c'=2] {'x'}, dimensions={0} | all-to-all | bytes 393216 | tf_op jit(solution)/shard_map/all_to_all | solution.py:33
  129.5 0.5 fusion.6
  130.0 0.1 slice.70
  130.1 12.2 %collective-permute-start.1 = (bf16[16,448]{1,0:T(8,128)(2,1)S(1)}, bf16[16,448]{1,0:T(8,128)(2,1)S(1)}, u32[]{:S(2)}, u32[]{:S(2)}) collective-permute-start(bf16[16,448]{1,0:T(8,128)(2,1)S(1)} %slice.70), channel_id=1, source_target_pairs={{0,1},{1,0},{2,3},{3,2},{4,5},{5,4},{6,7},{7,6},{8,9},{9,8},{10,11... | collective-permute-start | bytes 43016 | tf_op jit(solution)/shard_map/ppermute | solution.py:39
  142.3 0.8 collective-permute-done.1
  143.1 0.6 convert_multiply_fusion.2
  (17 shorter events, 0.4 us)
Async XLA Ops:
  7.2 0.7 copy-start
  7.2 93.0 %all-gather.2.cloned.1.call-start = ((), (), s32[]{:S(2)}) async-start(), calls=%async_computation.8 | async-start | bytes 3096576 | tf_op jit(solution)/shard_map/all_gather | solution.py:71
  9.6 13.2 %collective-permute-start = (bf16[16,448]{1,0:T(8,128)(2,1)S(1)}, bf16[16,448]{1,0:T(8,128)(2,1)S(1)}, u32[]{:S(2)}, u32[]{:S(2)}) collective-permute-start(bf16[16,448]{1,0:T(8,128)(2,1)S(1)} %get-tuple-element.21), channel_id=1, source_target_pairs={{0,1},{1,0},{2,3},{3,2},{4,5},{5,4},{6,7},{7,6},{8,9},{9,8},{10,11... | collective-permute-start | bytes 43016 | tf_op jit(solution)/shard_map/ppermute | solution.py:39
  63.4 9.3 %all-to-all-start.2 = ((bf16[4,128,192]{1,2,0:T(8,128)(2,1)}), bf16[4,128,192]{1,2,0:T(8,128)(2,1)S(1)}, u32[]{:S(2)}, u32[]{:S(2)}) async-start(bf16[4,128,192]{1,2,0:T(8,128)(2,1)} %broadcast_in_dim.74), calls=%async_computation.2 | async-start | bytes 393216 | tf_op jit(solution)/shard_map/all_to_all | solution.py:33
  74.7 14.2 %all-to-all-start.3 = ((f32[12,1,128]{2,1,0:T(1,128)}), f32[12,1,128]{2,1,0:T(1,128)S(1)}, u32[]{:S(2)}, u32[]{:S(2)}) async-start(f32[12,1,128]{2,1,0:T(1,128)} %broadcast_in_dim_broadcast_in_dim_broadcast_in_dim.2), calls=%async_computation.3 | async-start | bytes 12288 | tf_op jit(solution)/shard_map/all_to_all | solution.py:33
  100.2 2.6 %copy-start.1 = (bf16[1536,896]{1,0:T(8,128)(2,1)S(1)}, bf16[1536,896]{1,0:T(8,128)(2,1)}, u32[]{:S(2)}) copy-start(bf16[1536,896]{1,0:T(8,128)(2,1)} %all-gather.2.cloned.1.call-done) | copy-start | bytes 8257540
  130.1 13.0 %collective-permute-start.1 = (bf16[16,448]{1,0:T(8,128)(2,1)S(1)}, bf16[16,448]{1,0:T(8,128)(2,1)S(1)}, u32[]{:S(2)}, u32[]{:S(2)}) collective-permute-start(bf16[16,448]{1,0:T(8,128)(2,1)S(1)} %slice.70), channel_id=1, source_target_pairs={{0,1},{1,0},{2,3},{3,2},{4,5},{5,4},{6,7},{7,6},{8,9},{9,8},{10,11... | collective-permute-start | bytes 43016 | tf_op jit(solution)/shard_map/ppermute | solution.py:39
Sparse Core Ops, SparseCore 0:
  45.9 42.2 all-gather.1

commit v5 on v4

--- a/solution.py
+++ b/solution.py
@@ -18,6 +18,39 @@
 
 NZ, NY, NX, NC = 12, 8, 4, 2
 PACKED = 256
+TINY = 1e-30
+SMALL = 2.0**-34
+
+
+def polynomial():
+    def times(p, q):
+        out = [0.0] * (len(p) + len(q) - 1)
+        for i, a in enumerate(p):
+            for j, b in enumerate(q):
+                out[i + j] += a * b
+        return out
+
+    step = [FIRST_LIN, FIRST_CUBE]
+    inner = [0.0] + [SECOND_CUBE * v for v in times(step, step)]
+    inner[0] = SECOND_LIN
+    return times(step, inner)
+
+
+COEFS = polynomial()
+
+
+def expansion(coefs, at):
+    out = []
+    for order in range(len(coefs)):
+        value = 0.0
+        for power in range(len(coefs) - 1, order - 1, -1):
+            value = value * at + math.comb(power, order) * coefs[power]
+        out.append(value)
+    return out
+
+
+def along_z(value, shift):
+    return lax.ppermute(value, "z", [(z, (z + shift) % NZ) for z in range(NZ)])
 
 
 def three_parts(value):
@@ -73,31 +106,48 @@
     rows_later, same_y = lax.optimization_barrier((rows, same_y))
     same_z = spread(rows_later, "y", NY).reshape(-1, columns)
     block = sum_columns(rows_dot_t(same_z, same_y))
-    total_sq = jnp.broadcast_to(jnp.sum(block * block, keepdims=True), (1, 128))
-    total_sq = jnp.sum(spread(total_sq, "z", NZ), axis=0)
+    parts = three_parts(jnp.sum(block * block))
     block = block.astype(bf16).reshape(NY, -1, block.shape[1])
     held = block.shape[2]
-    shape = block.shape[:2] + (PACKED - held,)
-    lane = lax.broadcasted_iota(jnp.int32, shape, 2)
-    packed = jnp.zeros(shape, f32)
-    for k, part in enumerate(three_parts(total_sq[:, : shape[2]])):
-        packed = jnp.where(lane == k, part[None], packed)
+    lane = lax.broadcasted_iota(jnp.int32, block.shape[:2] + (PACKED - held,), 2)
+    packed = jnp.zeros(lane.shape, f32)
+    for k, part in enumerate(parts):
+        packed = jnp.where(lane == k, part, packed)
     block = jnp.concatenate([block, packed.astype(bf16)], axis=2)
     block = lax.all_to_all(block, "y", 0, 0)
     gram = jnp.concatenate([block[y, :, :held] for y in range(NY)], axis=1)
-    total_sq = jnp.sum(block[:, :1, held:].astype(f32))
-    scale_sq = lax.rsqrt(total_sq + EPSILON)
+    total_sq = jnp.broadcast_to(jnp.sum(block[:, :1, held:].astype(f32)), (8, 128))
+
+    row = lax.broadcasted_iota(jnp.int32, gram.shape, 0)
+    column = lax.broadcasted_iota(jnp.int32, gram.shape, 1)
+    place = lax.axis_index("y") * held + lax.axis_index("z") * gram.shape[0]
+    wide = gram.astype(f32)
+    diagonal = jnp.sum(jnp.where(column == place + row, wide, 0.0), axis=1, keepdims=True)
+    shift = jnp.sum(wide * wide, axis=1, keepdims=True) / jnp.maximum(diagonal, TINY)
+    weights = gram * SMALL
+    before = rows.astype(f32) * SMALL
+    terms = []
+    moving = [along_z(total_sq, step) for step in (1, 2)]
+    for phase in range(3):
+        product = rows_dot(weights, matrix)
+        terms.append(product)
+        before = product - shift * before
+        weights = rows_dot_t(before.astype(bf16), matrix)
+        if phase > 0:
+            total_sq, moving, weights = lax.optimization_barrier((total_sq, moving, weights))
+            total_sq = total_sq + sum(moving)
+        if phase == 1:
+            moving = [along_z(total_sq, step) for step in (3, 6, 9)]
+        weights = sum_columns(weights)
+    terms.append(rows_dot(weights, matrix))
+    scale_sq = lax.rsqrt(total_sq[:1, :1] + EPSILON)
     factor = jnp.sqrt(scale_sq)
-
-    first = (
-        factor * (FIRST_LIN * rows.astype(f32) + FIRST_CUBE * (scale_sq * rows_dot(gram, matrix)))
-    ).astype(bf16)
-    product = rows_dot(scale_sq * sum_columns(rows_dot_t(first, matrix)), matrix)
-    applied = (FIRST_LIN * first.astype(f32) + FIRST_CUBE * product).astype(bf16)
-    second = rows_dot(scale_sq * sum_columns(rows_dot_t(applied, matrix)), matrix).astype(bf16)
-    product = rows_dot(scale_sq * sum_columns(rows_dot_t(second, matrix)), matrix)
-    third = FIRST_LIN * second.astype(f32) + FIRST_CUBE * product
-    ortho = (SECOND_LIN * first.astype(f32) + SECOND_CUBE * third).astype(bf16)
+    taylor = expansion(COEFS[1:], scale_sq * shift)
+    tail = taylor[3] * terms[3]
+    for k in (2, 1, 0):
+        tail = scale_sq * tail + taylor[k] * terms[k]
+    tail = (scale_sq / SMALL) * tail
+    ortho = (factor * (COEFS[0] * rows.astype(f32) + tail)).astype(bf16)
 
     half = columns // 2
     other = swap(ortho[:, half:])

time: 151 us -> 165 us (1.093)
  blocking collectives: 71.4 us -> 38.6 us
  starting transfers between devices: 33.9 us -> 64 us
  waiting for transfers between devices: 15.6 us -> 23.6 us
  between operations: 14.9 us -> 19 us
  other arithmetic: 3.88 us -> 6.39 us
  local copies, waits for them, and re-layouts: 3.43 us -> 5.26 us
    all_to_all x5 -> x2, blocking collectives: 61.8 us -> 38.6 us  [spread(): lax.all_to_all(jnp.broadcast_to(block[None], (size,) + block.shape), axis...]
    ppermute x0 -> x5, starting transfers between devices: none -> 20.7 us  [along_z(): return lax.ppermute(value, 'z', [(z, (z + shift) % NZ) for z in range(NZ)])]
    all_to_all x1 -> x0, blocking collectives: 9.61 us -> none  [body(): block = lax.all_to_all(block, 'y', 0, 0)]
    all_to_all x0 -> x1, waiting for transfers between devices: none -> 7.3 us  [body(): block = lax.all_to_all(block, 'y', 0, 0)]
    all_to_all x2 -> x4, starting transfers between devices: 9.32 us -> 16.1 us  [spread(): lax.all_to_all(jnp.broadcast_to(block[None], (size,) + block.shape), axis...]
    ppermute x0 -> x5, waiting for transfers between devices: none -> 4.19 us  [along_z(): return lax.ppermute(value, 'z', [(z, (z + shift) % NZ) for z in range(NZ)])]
    all_to_all x2 -> x4, waiting for transfers between devices: 14 us -> 10.4 us  [spread(): lax.all_to_all(jnp.broadcast_to(block[None], (size,) + block.shape), axis...]
    all_to_all x0 -> x1, starting transfers between devices: none -> 3.35 us  [body(): block = lax.all_to_all(block, 'y', 0, 0)]
  transfers between devices with their start and end apart: 5 -> 13, of which waited for: 4 -> 7; matrix products, arithmetic and copies ran while one was open for 3% -> 6% of each run, Pallas kernels for 0% -> 0%
where the time goes in v5:
time: 165 us; the launch traced here: 164 us
  starting transfers between devices  64 us (39%)
  blocking collectives  38.6 us (23%)
  waiting for transfers between devices  23.6 us (14%)
  between operations  19 us (12%)
  matrix products  7.59 us (5%)
  other arithmetic  6.39 us (4%)
  local copies, waits for them, and re-layouts  5.26 us (3%)
    all_to_all x2, blocking collectives, spread(): lax.all_to_all(jnp.broadcast_to(block[None], (size,) + block.shape), axis...  38.6 us
    ppermute x2, starting transfers between devices, swap(): return lax.ppermute(block, 'c', [(0, 1), (1, 0)])  23.8 us
    ppermute x5, starting transfers between devices, along_z(): return lax.ppermute(value, 'z', [(z, (z + shift) % NZ) for z in range(NZ)])  20.7 us
    all_to_all x4, starting transfers between devices, spread(): lax.all_to_all(jnp.broadcast_to(block[None], (size,) + block.shape), axis...  16.1 us
    all_to_all x4, waiting for transfers between devices, spread(): lax.all_to_all(jnp.broadcast_to(block[None], (size,) + block.shape), axis...  10.4 us
    all_to_all x1, waiting for transfers between devices, body(): block = lax.all_to_all(block, 'y', 0, 0)  7.3 us
    ppermute x5, waiting for transfers between devices, along_z(): return lax.ppermute(value, 'z', [(z, (z + shift) % NZ) for z in range(NZ)])  4.19 us
    dot_general x4, matrix products, rows_dot(): jnp.dot(rows.astype(jnp.bfloat16), matrix, preferred_element_type=jnp.flo...  3.86 us
  transfers between devices with their start and end apart: 13, of which 7 were waited for; matrix products, arithmetic and copies ran while one was open for 6% of the time, Pallas kernels for 0%

profile of v5, /device:TPU:1, one launch (start us, length us, event | category | flops | bytes accessed | tf_op | source)
XLA Modules:
  0.0 164.4 jit_solution(11134226935976357698)
XLA Ops:
  7.2 0.0 copy-start
  7.2 0.0 all-gather.2.cloned.1.call-start
  7.2 0.6 copy-done
  7.8 0.2 dynamic-slice_reduce_fusion
  8.0 1.5 fusion.9
  9.6 12.4 %collective-permute-start = (bf16[16,448]{1,0:T(8,128)(2,1)S(1)}, bf16[16,448]{1,0:T(8,128)(2,1)S(1)}, u32[]{:S(2)}, u32[]{:S(2)}) collective-permute-start(bf16[16,448]{1,0:T(8,128)(2,1)S(1)} %get-tuple-element.45), channel_id=1, source_target_pairs={{0,1},{1,0},{2,3},{3,2},{4,5},{5,4},{6,7},{7,6},{8,9},{9,8},{10,11... | collective-permute-start | bytes 43016 | tf_op jit(solution)/shard_map/ppermute | solution.py:72
  21.9 0.8 collective-permute-done
  22.8 0.1 pad_maximum_fusion.1
  22.9 22.9 %all_to_all.35 = bf16[12,16,896]{2,1,0:T(8,128)(2,1)} all-to-all(bf16[12,16,896]{2,1,0:T(8,128)(2,1)S(1)} %broadcast_in_dim.33), channel_id=1, replica_groups=mesh['z'=12,'y'=8,'x'=4,'c'=2] {'z'}, dimensions={0} | all-to-all | bytes 688128 | tf_op jit(solution)/shard_map/all_to_all | solution.py:66
  45.8 0.0 all-gather.2.cloned.1.call-update
  45.9 15.6 %all_to_all.36 = bf16[8,16,896]{2,1,0:T(8,128)(2,1)S(1)} all-to-all(bf16[8,16,896]{2,1,0:T(8,128)(2,1)S(1)} %broadcast_in_dim.64), channel_id=1, replica_groups=mesh['z'=12,'y'=8,'x'=4,'c'=2] {'y'}, dimensions={0} | all-to-all | bytes 458752 | tf_op jit(solution)/shard_map/all_to_all | solution.py:66
  61.5 1.2 convolution_convert_fusion.3
  62.7 0.7 broadcast_in_dim.65
  63.4 4.0 %all-to-all-start.2 = ((bf16[4,128,192]{1,2,0:T(8,128)(2,1)}), bf16[4,128,192]{1,2,0:T(8,128)(2,1)S(1)}, u32[]{:S(2)}, u32[]{:S(2)}) async-start(bf16[4,128,192]{1,2,0:T(8,128)(2,1)} %broadcast_in_dim.65), calls=%async_computation.2 | async-start | bytes 393216 | tf_op jit(solution)/shard_map/all_to_all | solution.py:66
  67.5 5.2 %all-to-all-done.2 = bf16[4,128,192]{1,2,0:T(8,128)(2,1)S(1)} async-done(((bf16[4,128,192]{1,2,0:T(8,128)(2,1)}), bf16[4,128,192]{1,2,0:T(8,128)(2,1)S(1)}, u32[]{:S(2)}, u32[]{:S(2)}) %all-to-all-start.2) | async-done | bytes 196640 | tf_op jit(solution)/shard_map/all_to_all | solution.py:66
  72.7 0.6 fusion.24
  73.4 0.1 copy.14
  77.5 0.6 compare_select_fusion
  78.1 1.2 select_convert_fusion
  79.3 0.7 pad_maximum_fusion
  80.0 3.4 %all-to-all-start.3 = ((bf16[8,16,256]{2,1,0:T(8,128)(2,1)}), bf16[8,16,256]{2,1,0:T(8,128)(2,1)S(1)}, u32[]{:S(2)}, u32[]{:S(2)}) async-start(bf16[8,16,256]{2,1,0:T(8,128)(2,1)} %pad_maximum_fusion), calls=%async_computation.3 | async-start | bytes 131072 | tf_op jit(solution)/shard_map/all_to_all | solution.py:117
  83.4 7.3 %all-to-all-done.3 = bf16[8,16,256]{2,1,0:T(8,128)(2,1)S(1)} async-done(((bf16[8,16,256]{2,1,0:T(8,128)(2,1)}), bf16[8,16,256]{2,1,0:T(8,128)(2,1)S(1)}, u32[]{:S(2)}, u32[]{:S(2)}) %all-to-all-start.3) | async-done | bytes 65568 | tf_op jit(solution)/shard_map/all_to_all | solution.py:117
  90.7 0.1 concatenate.11
  90.8 0.2 fusion.8
  91.0 0.0 all-gather.2.cloned.1.call-done
  91.0 0.0 copy-start.1
  91.0 2.4 %fusion.14 = f32[16,896]{1,0:T(8,128)S(1)} fusion(bf16[1536,896]{1,0:T(8,128)(2,1)} %all-gather.2.cloned.1.call-done, bf16[16,1536]{1,0:T(8,128)(2,1)S(1)} %concatenate.11), kind=kOutput, calls=%fused_computation.34 | convolution fusion | flops 44064768 | bytes 2859008 | tf_op jit(solution)/shard_map/dot_general | solution.py:86
  93.4 0.2 copy-done.1
  93.6 0.8 convolution_convert_fusion.2
  94.4 0.7 broadcast_in_dim.72
  95.1 3.4 %all-to-all-start.4 = ((bf16[4,16,1536]{2,1,0:T(8,128)(2,1)}), bf16[4,16,1536]{2,1,0:T(8,128)(2,1)S(1)}, u32[]{:S(2)}, u32[]{:S(2)}) async-start(bf16[4,16,1536]{2,1,0:T(8,128)(2,1)} %broadcast_in_dim.72), calls=%async_computation.4 | async-start | bytes 393216 | tf_op jit(solution)/shard_map/all_to_all | solution.py:66
  98.5 0.7 fusion.22
  99.2 0.6 broadcast_in_dim.70
  99.8 5.6 %collective-permute-start.1 = (f32[8,128]{1,0:T(8,128)S(1)}, f32[8,128]{1,0:T(8,128)S(1)}, u32[]{:S(2)}, u32[]{:S(2)}) collective-permute-start(f32[8,128]{1,0:T(8,128)S(1)} %broadcast_in_dim.70), channel_id=1, source_target_pairs={{0,64},{64,128},{128,192},{192,256},{256,320},{320,384},{384,448},... | collective-permute-start | bytes 12296 | tf_op jit(solution)/shard_map/ppermute | solution.py:53
  105.4 1.9 %collective-permute-start.2 = (f32[8,128]{1,0:T(8,128)S(1)}, f32[8,128]{1,0:T(8,128)S(1)}, u32[]{:S(2)}, u32[]{:S(2)}) collective-permute-start(f32[8,128]{1,0:T(8,128)S(1)} %broadcast_in_dim.70), channel_id=1, source_target_pairs={{0,128},{64,192},{128,256},{192,320},{256,384},{320,448},{384,512}... | collective-permute-start | bytes 12296 | tf_op jit(solution)/shard_map/ppermute | solution.py:53
  107.3 0.0 all-to-all-done.4
  107.4 0.5 fusion.25
  107.9 0.8 convolution_convert_fusion.1
  108.7 0.0 collective-permute-done.1
  108.7 3.2 %collective-permute-done.2 = f32[8,128]{1,0:T(8,128)S(1)} collective-permute-done((f32[8,128]{1,0:T(8,128)S(1)}, f32[8,128]{1,0:T(8,128)S(1)}, u32[]{:S(2)}, u32[]{:S(2)}) %collective-permute-start.2) | collective-permute-done | bytes 4128 | tf_op jit(solution)/shard_map/ppermute | solution.py:53
  111.9 0.7 broadcast_in_dim.73
  112.6 4.2 %all-to-all-start.5 = ((bf16[4,16,1536]{2,1,0:T(8,128)(2,1)}), bf16[4,16,1536]{2,1,0:T(8,128)(2,1)S(1)}, u32[]{:S(2)}, u32[]{:S(2)}) async-start(bf16[4,16,1536]{2,1,0:T(8,128)(2,1)} %broadcast_in_dim.73), calls=%async_computation.5 | async-start | bytes 393216 | tf_op jit(solution)/shard_map/all_to_all | solution.py:66
  116.8 2.4 %collective-permute-start.3 = (f32[8,128]{1,0:T(8,128)S(1)}, f32[8,128]{1,0:T(8,128)S(1)}, u32[]{:S(2)}, u32[]{:S(2)}) collective-permute-start(f32[8,128]{1,0:T(8,128)S(1)} %add_add_fusion.1), channel_id=1, source_target_pairs={{0,192},{64,256},{128,320},{192,384},{256,448},{320,512},{384,576}... | collective-permute-start | bytes 12296 | tf_op jit(solution)/shard_map/ppermute | solution.py:53
  119.2 7.0 %collective-permute-start.4 = (f32[8,128]{1,0:T(8,128)S(1)}, f32[8,128]{1,0:T(8,128)S(1)}, u32[]{:S(2)}, u32[]{:S(2)}) collective-permute-start(f32[8,128]{1,0:T(8,128)S(1)} %add_add_fusion.1), channel_id=1, source_target_pairs={{0,384},{64,448},{128,512},{192,576},{256,640},{320,704},{384,0},{... | collective-permute-start | bytes 12296 | tf_op jit(solution)/shard_map/ppermute | solution.py:53
  126.3 3.8 %collective-permute-start.5 = (f32[8,128]{1,0:T(8,128)S(1)}, f32[8,128]{1,0:T(8,128)S(1)}, u32[]{:S(2)}, u32[]{:S(2)}) collective-permute-start(f32[8,128]{1,0:T(8,128)S(1)} %add_add_fusion.1), channel_id=1, source_target_pairs={{0,576},{64,640},{128,704},{192,0},{256,64},{320,128},{384,192},{4... | collective-permute-start | bytes 12296 | tf_op jit(solution)/shard_map/ppermute | solution.py:53
  130.0 0.0 all-to-all-done.5
  130.1 0.5 fusion.26
  130.5 0.8 convolution_convert_fusion
  131.4 0.0 collective-permute-done.3
  131.4 0.0 collective-permute-done.4
  131.4 1.0 collective-permute-done.5
  132.4 0.5 slice.55
  133.7 0.7 broadcast_in_dim.74
  134.4 4.5 %all-to-all-start.6 = ((bf16[4,16,1536]{2,1,0:T(8,128)(2,1)}), bf16[4,16,1536]{2,1,0:T(8,128)(2,1)S(1)}, u32[]{:S(2)}, u32[]{:S(2)}) async-start(bf16[4,16,1536]{2,1,0:T(8,128)(2,1)} %broadcast_in_dim.74), calls=%async_computation.6 | async-start | bytes 393216 | tf_op jit(solution)/shard_map/all_to_all | solution.py:66
  138.9 5.2 %all-to-all-done.6 = bf16[4,16,1536]{2,1,0:T(8,128)(2,1)S(1)} async-done(((bf16[4,16,1536]{2,1,0:T(8,128)(2,1)}), bf16[4,16,1536]{2,1,0:T(8,128)(2,1)S(1)}, u32[]{:S(2)}, u32[]{:S(2)}) %all-to-all-start.6) | async-done | bytes 196640 | tf_op jit(solution)/shard_map/all_to_all | solution.py:66
  144.1 0.5 fusion.13
  144.6 0.1 slice.70
  144.7 11.4 %collective-permute-start.6 = (bf16[16,448]{1,0:T(8,128)(2,1)S(1)}, bf16[16,448]{1,0:T(8,128)(2,1)S(1)}, u32[]{:S(2)}, u32[]{:S(2)}) collective-permute-start(bf16[16,448]{1,0:T(8,128)(2,1)S(1)} %slice.70), channel_id=1, source_target_pairs={{0,1},{1,0},{2,3},{3,2},{4,5},{5,4},{6,7},{7,6},{8,9},{9,8},{10,11... | collective-permute-start | bytes 43016 | tf_op jit(solution)/shard_map/ppermute | solution.py:72
  156.1 0.8 collective-permute-done.6
  157.0 0.6 convert_multiply_fusion.3
  (16 shorter events, 0.2 us)
Async XLA Ops:
  7.2 0.7 copy-start
  7.2 83.8 %all-gather.2.cloned.1.call-start = ((), (), s32[]{:S(2)}) async-start(), calls=%async_computation.7 | async-start | bytes 3096576 | tf_op jit(solution)/shard_map/all_gather | solution.py:104
  9.6 13.2 %collective-permute-start = (bf16[16,448]{1,0:T(8,128)(2,1)S(1)}, bf16[16,448]{1,0:T(8,128)(2,1)S(1)}, u32[]{:S(2)}, u32[]{:S(2)}) collective-permute-start(bf16[16,448]{1,0:T(8,128)(2,1)S(1)} %get-tuple-element.45), channel_id=1, source_target_pairs={{0,1},{1,0},{2,3},{3,2},{4,5},{5,4},{6,7},{7,6},{8,9},{9,8},{10,11... | collective-permute-start | bytes 43016 | tf_op jit(solution)/shard_map/ppermute | solution.py:72
  63.4 9.3 %all-to-all-start.2 = ((bf16[4,128,192]{1,2,0:T(8,128)(2,1)}), bf16[4,128,192]{1,2,0:T(8,128)(2,1)S(1)}, u32[]{:S(2)}, u32[]{:S(2)}) async-start(bf16[4,128,192]{1,2,0:T(8,128)(2,1)} %broadcast_in_dim.65), calls=%async_computation.2 | async-start | bytes 393216 | tf_op jit(solution)/shard_map/all_to_all | solution.py:66
  80.0 10.7 %all-to-all-start.3 = ((bf16[8,16,256]{2,1,0:T(8,128)(2,1)}), bf16[8,16,256]{2,1,0:T(8,128)(2,1)S(1)}, u32[]{:S(2)}, u32[]{:S(2)}) async-start(bf16[8,16,256]{2,1,0:T(8,128)(2,1)} %pad_maximum_fusion), calls=%async_computation.3 | async-start | bytes 131072 | tf_op jit(solution)/shard_map/all_to_all | solution.py:117
  91.0 2.6 %copy-start.1 = (bf16[1536,896]{1,0:T(8,128)(2,1)S(1)}, bf16[1536,896]{1,0:T(8,128)(2,1)}, u32[]{:S(2)}) copy-start(bf16[1536,896]{1,0:T(8,128)(2,1)} %all-gather.2.cloned.1.call-done) | copy-start | bytes 8257540
  95.1 12.2 %all-to-all-start.4 = ((bf16[4,16,1536]{2,1,0:T(8,128)(2,1)}), bf16[4,16,1536]{2,1,0:T(8,128)(2,1)S(1)}, u32[]{:S(2)}, u32[]{:S(2)}) async-start(bf16[4,16,1536]{2,1,0:T(8,128)(2,1)} %broadcast_in_dim.72), calls=%async_computation.4 | async-start | bytes 393216 | tf_op jit(solution)/shard_map/all_to_all | solution.py:66
  99.8 8.9 %collective-permute-start.1 = (f32[8,128]{1,0:T(8,128)S(1)}, f32[8,128]{1,0:T(8,128)S(1)}, u32[]{:S(2)}, u32[]{:S(2)}) collective-permute-start(f32[8,128]{1,0:T(8,128)S(1)} %broadcast_in_dim.70), channel_id=1, source_target_pairs={{0,64},{64,128},{128,192},{192,256},{256,320},{320,384},{384,448},... | collective-permute-start | bytes 12296 | tf_op jit(solution)/shard_map/ppermute | solution.py:53
  105.4 6.5 %collective-permute-start.2 = (f32[8,128]{1,0:T(8,128)S(1)}, f32[8,128]{1,0:T(8,128)S(1)}, u32[]{:S(2)}, u32[]{:S(2)}) collective-permute-start(f32[8,128]{1,0:T(8,128)S(1)} %broadcast_in_dim.70), channel_id=1, source_target_pairs={{0,128},{64,192},{128,256},{192,320},{256,384},{320,448},{384,512}... | collective-permute-start | bytes 12296 | tf_op jit(solution)/shard_map/ppermute | solution.py:53
  112.6 17.5 %all-to-all-start.5 = ((bf16[4,16,1536]{2,1,0:T(8,128)(2,1)}), bf16[4,16,1536]{2,1,0:T(8,128)(2,1)S(1)}, u32[]{:S(2)}, u32[]{:S(2)}) async-start(bf16[4,16,1536]{2,1,0:T(8,128)(2,1)} %broadcast_in_dim.73), calls=%async_computation.5 | async-start | bytes 393216 | tf_op jit(solution)/shard_map/all_to_all | solution.py:66
  116.8 14.6 %collective-permute-start.3 = (f32[8,128]{1,0:T(8,128)S(1)}, f32[8,128]{1,0:T(8,128)S(1)}, u32[]{:S(2)}, u32[]{:S(2)}) collective-permute-start(f32[8,128]{1,0:T(8,128)S(1)} %add_add_fusion.1), channel_id=1, source_target_pairs={{0,192},{64,256},{128,320},{192,384},{256,448},{320,512},{384,576}... | collective-permute-start | bytes 12296 | tf_op jit(solution)/shard_map/ppermute | solution.py:53
  119.2 12.2 %collective-permute-start.4 = (f32[8,128]{1,0:T(8,128)S(1)}, f32[8,128]{1,0:T(8,128)S(1)}, u32[]{:S(2)}, u32[]{:S(2)}) collective-permute-start(f32[8,128]{1,0:T(8,128)S(1)} %add_add_fusion.1), channel_id=1, source_target_pairs={{0,384},{64,448},{128,512},{192,576},{256,640},{320,704},{384,0},{... | collective-permute-start | bytes 12296 | tf_op jit(solution)/shard_map/ppermute | solution.py:53
  126.3 6.2 %collective-permute-start.5 = (f32[8,128]{1,0:T(8,128)S(1)}, f32[8,128]{1,0:T(8,128)S(1)}, u32[]{:S(2)}, u32[]{:S(2)}) collective-permute-start(f32[8,128]{1,0:T(8,128)S(1)} %add_add_fusion.1), channel_id=1, source_target_pairs={{0,576},{64,640},{128,704},{192,0},{256,64},{320,128},{384,192},{4... | collective-permute-start | bytes 12296 | tf_op jit(solution)/shard_map/ppermute | solution.py:53
  134.4 9.7 %all-to-all-start.6 = ((bf16[4,16,1536]{2,1,0:T(8,128)(2,1)}), bf16[4,16,1536]{2,1,0:T(8,128)(2,1)S(1)}, u32[]{:S(2)}, u32[]{:S(2)}) async-start(bf16[4,16,1536]{2,1,0:T(8,128)(2,1)} %broadcast_in_dim.74), calls=%async_computation.6 | async-start | bytes 393216 | tf_op jit(solution)/shard_map/all_to_all | solution.py:66
  144.7 12.3 %collective-permute-start.6 = (bf16[16,448]{1,0:T(8,128)(2,1)S(1)}, bf16[16,448]{1,0:T(8,128)(2,1)S(1)}, u32[]{:S(2)}, u32[]{:S(2)}) collective-permute-start(bf16[16,448]{1,0:T(8,128)(2,1)S(1)} %slice.70), channel_id=1, source_target_pairs={{0,1},{1,0},{2,3},{3,2},{4,5},{5,4},{6,7},{7,6},{8,9},{9,8},{10,11... | collective-permute-start | bytes 43016 | tf_op jit(solution)/shard_map/ppermute | solution.py:72
Sparse Core Ops, SparseCore 0:
  45.9 42.3 all-gather.1

commit v6 on v4

--- a/solution.py
+++ b/solution.py
@@ -73,25 +73,26 @@
     rows_later, same_y = lax.optimization_barrier((rows, same_y))
     same_z = spread(rows_later, "y", NY).reshape(-1, columns)
     block = sum_columns(rows_dot_t(same_z, same_y))
-    total_sq = jnp.broadcast_to(jnp.sum(block * block, keepdims=True), (1, 128))
-    total_sq = jnp.sum(spread(total_sq, "z", NZ), axis=0)
+    squares = jnp.sum(block * block, axis=0, keepdims=True)
     block = block.astype(bf16).reshape(NY, -1, block.shape[1])
     held = block.shape[2]
-    shape = block.shape[:2] + (PACKED - held,)
-    lane = lax.broadcasted_iota(jnp.int32, shape, 2)
-    packed = jnp.zeros(shape, f32)
-    for k, part in enumerate(three_parts(total_sq[:, : shape[2]])):
-        packed = jnp.where(lane == k, part[None], packed)
-    block = jnp.concatenate([block, packed.astype(bf16)], axis=2)
-    block = lax.all_to_all(block, "y", 0, 0)
+    spare = PACKED - held
+    squares = sum(squares[:, k : k + spare] for k in range(0, held, spare))
+    line = lax.broadcasted_iota(jnp.int32, (block.shape[1], spare), 0)
+    packed = jnp.zeros(line.shape, f32)
+    for k, part in enumerate(three_parts(squares)):
+        packed = jnp.where(line == k, part, packed)
+    packed = jnp.broadcast_to(packed.astype(bf16), (NY,) + packed.shape)
+    block = lax.all_to_all(jnp.concatenate([block, packed], axis=2), "y", 0, 0)
     gram = jnp.concatenate([block[y, :, :held] for y in range(NY)], axis=1)
-    total_sq = jnp.sum(block[:, :1, held:].astype(f32))
+    squares = jnp.sum(block[:, :, held:].astype(f32), axis=(0, 1))[None]
+    squares = spread(jnp.concatenate([squares, jnp.zeros_like(squares)], axis=1), "z", NZ)
+    product = rows_dot(gram, matrix)
+    product, squares = lax.optimization_barrier((product, squares))
+    total_sq = jnp.sum(squares)
     scale_sq = lax.rsqrt(total_sq + EPSILON)
     factor = jnp.sqrt(scale_sq)
-
-    first = (
-        factor * (FIRST_LIN * rows.astype(f32) + FIRST_CUBE * (scale_sq * rows_dot(gram, matrix)))
-    ).astype(bf16)
+    first = (factor * (FIRST_LIN * rows.astype(f32) + (FIRST_CUBE * scale_sq) * product)).astype(bf16)
     product = rows_dot(scale_sq * sum_columns(rows_dot_t(first, matrix)), matrix)
     applied = (FIRST_LIN * first.astype(f32) + FIRST_CUBE * product).astype(bf16)
     second = rows_dot(scale_sq * sum_columns(rows_dot_t(applied, matrix)), matrix).astype(bf16)

time: 151 us -> 148 us (0.980)
  waiting for transfers between devices: 15.6 us -> 13.2 us
    all_to_all x2, waiting for transfers between devices: 14 us -> 11.5 us  [spread(): lax.all_to_all(jnp.broadcast_to(block[None], (size,) + block.shape), axis...]
  transfers between devices with their start and end apart: 5 -> 5, of which waited for: 4 -> 4; matrix products, arithmetic and copies ran while one was open for 3% -> 4% of each run, Pallas kernels for 0% -> 0%
where the time goes in v6:
time: 148 us
  blocking collectives  72.1 us (49%)
  starting transfers between devices  33.8 us (23%)
  between operations  14.9 us (10%)
  waiting for transfers between devices  13.2 us (9%)
  matrix products  7.4 us (5%)
  other arithmetic  3.52 us (2%)
  local copies, waits for them, and re-layouts  2.59 us (2%)
    all_to_all x5, blocking collectives, spread(): lax.all_to_all(jnp.broadcast_to(block[None], (size,) + block.shape), axis...  61.6 us
    ppermute x2, starting transfers between devices, swap(): return lax.ppermute(block, 'c', [(0, 1), (1, 0)])  24.4 us
    all_to_all x2, waiting for transfers between devices, spread(): lax.all_to_all(jnp.broadcast_to(block[None], (size,) + block.shape), axis...  11.5 us
    all_to_all x1, blocking collectives, body(): block = lax.all_to_all(jnp.concatenate([block, packed], axis=2), 'y', 0, 0)  10.4 us
    all_to_all x2, starting transfers between devices, spread(): lax.all_to_all(jnp.broadcast_to(block[None], (size,) + block.shape), axis...  9.34 us
    dot_general x4, matrix products, rows_dot_t(): lax.dot_general(rows, matrix, (((1,), (1,)), ((), ())), preferred_element...  4.05 us
    dot_general x3, matrix products, rows_dot(): jnp.dot(rows.astype(jnp.bfloat16), matrix, preferred_element_type=jnp.flo...  3.35 us
  transfers between devices with their start and end apart: 5, of which 4 were waited for; matrix products, arithmetic and copies ran while one was open for 4% of the time, Pallas kernels for 0%

profile of v6, /device:TPU:1, one launch (start us, length us, event | category | flops | bytes accessed | tf_op | source)
XLA Modules:
  0.0 147.5 jit_solution(2365888462301112084)
XLA Ops:
  7.2 0.0 copy-start
  7.2 0.0 all-gather.2.cloned.1.call-start
  7.2 0.6 copy-done
  7.8 0.2 dynamic-slice_reduce_fusion
  8.0 1.5 %fusion.6 = (bf16[2,16,448]{2,1,0:T(8,128)(2,1)S(1)}, f32[2,16,448]{2,1,0:T(8,128)}) fusion(f32[2,16,448]{2,1,0:T(8,128)} %param.3, s32[2]{0:T(128)S(1)} %dynamic-slice_reduce_fusion, f32[2,16,448]{2,1,0:T(8,128)} %param.4), kind=kLoop, calls=%fused_computation.29 | loop fusion | flops 100352 | bytes 200712 | tf_op jit(solution)/shard_map/jit(_where)/select_n | solution.py:64
  9.6 12.4 %collective-permute-start = (bf16[16,448]{1,0:T(8,128)(2,1)S(1)}, bf16[16,448]{1,0:T(8,128)(2,1)S(1)}, u32[]{:S(2)}, u32[]{:S(2)}) collective-permute-start(bf16[16,448]{1,0:T(8,128)(2,1)S(1)} %get-tuple-element.27), channel_id=1, source_target_pairs={{0,1},{1,0},{2,3},{3,2},{4,5},{5,4},{6,7},{7,6},{8,9},{9,8},{10,11... | collective-permute-start | bytes 43016 | tf_op jit(solution)/shard_map/ppermute | solution.py:39
  21.9 0.8 collective-permute-done
  22.8 0.1 pad_maximum_fusion.1
  22.9 22.9 %all_to_all.40 = bf16[12,16,896]{2,1,0:T(8,128)(2,1)} all-to-all(bf16[12,16,896]{2,1,0:T(8,128)(2,1)S(1)} %broadcast_in_dim.86), channel_id=1, replica_groups=mesh['z'=12,'y'=8,'x'=4,'c'=2] {'z'}, dimensions={0} | all-to-all | bytes 688128 | tf_op jit(solution)/shard_map/all_to_all | solution.py:33
  45.8 0.0 all-gather.2.cloned.1.call-update
  45.9 15.6 %all_to_all.41 = bf16[8,16,896]{2,1,0:T(8,128)(2,1)S(1)} all-to-all(bf16[8,16,896]{2,1,0:T(8,128)(2,1)S(1)} %broadcast_in_dim.87), channel_id=1, replica_groups=mesh['z'=12,'y'=8,'x'=4,'c'=2] {'y'}, dimensions={0} | all-to-all | bytes 458752 | tf_op jit(solution)/shard_map/all_to_all | solution.py:33
  61.5 1.2 convolution_convert_fusion.3
  62.7 0.7 broadcast_in_dim.88
  63.4 4.0 %all-to-all-start.2 = ((bf16[4,128,192]{1,2,0:T(8,128)(2,1)}), bf16[4,128,192]{1,2,0:T(8,128)(2,1)S(1)}, u32[]{:S(2)}, u32[]{:S(2)}) async-start(bf16[4,128,192]{1,2,0:T(8,128)(2,1)} %broadcast_in_dim.88), calls=%async_computation.2 | async-start | bytes 393216 | tf_op jit(solution)/shard_map/all_to_all | solution.py:33
  67.5 5.2 %all-to-all-done.2 = bf16[4,128,192]{1,2,0:T(8,128)(2,1)S(1)} async-done(((bf16[4,128,192]{1,2,0:T(8,128)(2,1)}), bf16[4,128,192]{1,2,0:T(8,128)(2,1)S(1)}, u32[]{:S(2)}, u32[]{:S(2)}) %all-to-all-start.2) | async-done | bytes 196640 | tf_op jit(solution)/shard_map/all_to_all | solution.py:33
  72.7 0.1 fusion.17
  72.8 0.1 copy.14
  73.0 0.1 fusion.14
  73.0 0.1 select_convert_fusion
  73.1 0.1 pad_maximum_fusion
  73.2 10.4 %all_to_all.42 = bf16[8,16,256]{2,1,0:T(8,128)(2,1)S(1)} all-to-all(bf16[8,16,256]{2,1,0:T(8,128)(2,1)S(1)} %pad_maximum_fusion), channel_id=1, replica_groups=mesh['z'=12,'y'=8,'x'=4,'c'=2] {'y'}, dimensions={0} | all-to-all | bytes 131072 | tf_op jit(solution)/shard_map/all_to_all | solution.py:86
  83.7 0.1 convert_reduce_fusion.4
  83.8 0.6 broadcast_in_dim.100
  84.4 5.3 %all-to-all-start.4 = ((f32[12,1,128]{2,1,0:T(1,128)}), f32[12,1,128]{2,1,0:T(1,128)S(1)}, u32[]{:S(2)}, u32[]{:S(2)}) async-start(f32[12,1,128]{2,1,0:T(1,128)} %broadcast_in_dim.100), calls=%async_computation.4 | async-start | bytes 12288 | tf_op jit(solution)/shard_map/all_to_all | solution.py:33
  89.7 0.1 concatenate.14
  89.8 0.0 all-gather.2.cloned.1.call-done
  89.8 0.0 copy-start.1
  89.8 2.4 %fusion.18 = f32[16,896]{1,0:T(8,128)S(1)} fusion(bf16[16,1536]{1,0:T(8,128)(2,1)S(1)} %concatenate.14, bf16[1536,896]{1,0:T(8,128)(2,1)} %all-gather.2.cloned.1.call-done), kind=kOutput, calls=%fused_computation.66 | convolution fusion | flops 44040192 | bytes 2859008 | tf_op jit(solution)/shard_map/dot_general | solution.py:53
  92.2 6.3 %all-to-all-done.4 = f32[12,1,128]{2,1,0:T(1,128)S(1)} async-done(((f32[12,1,128]{2,1,0:T(1,128)}), f32[12,1,128]{2,1,0:T(1,128)S(1)}, u32[]{:S(2)}, u32[]{:S(2)}) %all-to-all-start.4) | async-done | bytes 6176 | tf_op jit(solution)/shard_map/all_to_all | solution.py:33
  98.6 0.6 reduce_sum.66
  99.9 0.1 multiply_convert_fusion.3
  100.0 0.0 copy-done.1
  100.0 0.8 convolution_convert_fusion.2
  100.8 7.5 %all_to_all.43 = bf16[4,16,1536]{2,1,0:T(8,128)(2,1)S(1)} all-to-all(bf16[4,16,1536]{2,1,0:T(8,128)(2,1)S(1)} %broadcast_in_dim.101), channel_id=1, replica_groups=mesh['z'=12,'y'=8,'x'=4,'c'=2] {'x'}, dimensions={0} | all-to-all | bytes 393216 | tf_op jit(solution)/shard_map/all_to_all | solution.py:33
  108.4 1.2 convolution_convert_fusion.1
  109.6 7.5 %all_to_all.44 = bf16[4,16,1536]{2,1,0:T(8,128)(2,1)S(1)} all-to-all(bf16[4,16,1536]{2,1,0:T(8,128)(2,1)S(1)} %broadcast_in_dim.102), channel_id=1, replica_groups=mesh['z'=12,'y'=8,'x'=4,'c'=2] {'x'}, dimensions={0} | all-to-all | bytes 393216 | tf_op jit(solution)/shard_map/all_to_all | solution.py:33
  117.2 0.5 convolution_convert_fusion.4
  117.7 0.8 convolution_convert_fusion
  118.6 8.0 %all_to_all.45 = bf16[4,16,1536]{2,1,0:T(8,128)(2,1)S(1)} all-to-all(bf16[4,16,1536]{2,1,0:T(8,128)(2,1)S(1)} %broadcast_in_dim.103), channel_id=1, replica_groups=mesh['z'=12,'y'=8,'x'=4,'c'=2] {'x'}, dimensions={0} | all-to-all | bytes 393216 | tf_op jit(solution)/shard_map/all_to_all | solution.py:33
  126.6 0.5 fusion.5
  127.1 0.1 slice.81
  127.1 12.1 %collective-permute-start.1 = (bf16[16,448]{1,0:T(8,128)(2,1)S(1)}, bf16[16,448]{1,0:T(8,128)(2,1)S(1)}, u32[]{:S(2)}, u32[]{:S(2)}) collective-permute-start(bf16[16,448]{1,0:T(8,128)(2,1)S(1)} %slice.81), channel_id=1, source_target_pairs={{0,1},{1,0},{2,3},{3,2},{4,5},{5,4},{6,7},{7,6},{8,9},{9,8},{10,11... | collective-permute-start | bytes 43016 | tf_op jit(solution)/shard_map/ppermute | solution.py:39
  139.2 0.8 collective-permute-done.1
  140.0 0.6 convert_multiply_fusion.2
  (17 shorter events, 0.3 us)
Async XLA Ops:
  7.2 0.7 copy-start
  7.2 82.6 %all-gather.2.cloned.1.call-start = ((), (), s32[]{:S(2)}) async-start(), calls=%async_computation.8 | async-start | bytes 3096576 | tf_op jit(solution)/shard_map/all_gather | solution.py:71
  9.6 13.2 %collective-permute-start = (bf16[16,448]{1,0:T(8,128)(2,1)S(1)}, bf16[16,448]{1,0:T(8,128)(2,1)S(1)}, u32[]{:S(2)}, u32[]{:S(2)}) collective-permute-start(bf16[16,448]{1,0:T(8,128)(2,1)S(1)} %get-tuple-element.27), channel_id=1, source_target_pairs={{0,1},{1,0},{2,3},{3,2},{4,5},{5,4},{6,7},{7,6},{8,9},{9,8},{10,11... | collective-permute-start | bytes 43016 | tf_op jit(solution)/shard_map/ppermute | solution.py:39
  63.4 9.3 %all-to-all-start.2 = ((bf16[4,128,192]{1,2,0:T(8,128)(2,1)}), bf16[4,128,192]{1,2,0:T(8,128)(2,1)S(1)}, u32[]{:S(2)}, u32[]{:S(2)}) async-start(bf16[4,128,192]{1,2,0:T(8,128)(2,1)} %broadcast_in_dim.88), calls=%async_computation.2 | async-start | bytes 393216 | tf_op jit(solution)/shard_map/all_to_all | solution.py:33
  84.4 14.2 %all-to-all-start.4 = ((f32[12,1,128]{2,1,0:T(1,128)}), f32[12,1,128]{2,1,0:T(1,128)S(1)}, u32[]{:S(2)}, u32[]{:S(2)}) async-start(f32[12,1,128]{2,1,0:T(1,128)} %broadcast_in_dim.100), calls=%async_computation.4 | async-start | bytes 12288 | tf_op jit(solution)/shard_map/all_to_all | solution.py:33
  89.8 10.2 %copy-start.1 = (bf16[1536,896]{1,0:T(8,128)(2,1)S(1)}, bf16[1536,896]{1,0:T(8,128)(2,1)}, u32[]{:S(2)}) copy-start(bf16[1536,896]{1,0:T(8,128)(2,1)} %all-gather.2.cloned.1.call-done) | copy-start | bytes 8257540
  127.1 12.9 %collective-permute-start.1 = (bf16[16,448]{1,0:T(8,128)(2,1)S(1)}, bf16[16,448]{1,0:T(8,128)(2,1)S(1)}, u32[]{:S(2)}, u32[]{:S(2)}) collective-permute-start(bf16[16,448]{1,0:T(8,128)(2,1)S(1)} %slice.81), channel_id=1, source_target_pairs={{0,1},{1,0},{2,3},{3,2},{4,5},{5,4},{6,7},{7,6},{8,9},{9,8},{10,11... | collective-permute-start | bytes 43016 | tf_op jit(solution)/shard_map/ppermute | solution.py:39
Sparse Core Ops, SparseCore 0:
  45.9 43.4 all-gather.1

commit v7 on v6

--- a/solution.py
+++ b/solution.py
@@ -59,14 +59,14 @@
     rounded = (grad + MOMENTUM_COEF * new_momentum).astype(bf16)
     dp = lax.axis_index("z") * NY + lax.axis_index("y")
     core = lax.axis_index("c")
-    own_lengths = lax.dynamic_index_in_dim(lengths, dp, 1, keepdims=False)
-    slots = lax.broadcasted_iota(jnp.int32, rounded.shape, 1)
-    rounded = jnp.where(slots < own_lengths[:, None, None], rounded, jnp.zeros_like(rounded))
     first_core = core == 0
     mine = jnp.where(first_core, rounded[0], rounded[1])
     theirs = jnp.where(first_core, rounded[1], rounded[0])
     rows = jnp.concatenate([mine, swap(theirs)], axis=1)
     columns = rows.shape[1]
+    own_length = lax.dynamic_slice(lengths, (core, dp), (1, 1))
+    slots = lax.broadcasted_iota(jnp.int32, rows.shape, 0)
+    rows = jnp.where(slots < own_length, rows, jnp.zeros_like(rows))
     same_y = spread(rows, "z", NZ).reshape(-1, columns)
     matrix = lax.all_gather(same_y, "y", axis=0, tiled=True)
 
@@ -78,10 +78,9 @@
     held = block.shape[2]
     spare = PACKED - held
     squares = sum(squares[:, k : k + spare] for k in range(0, held, spare))
-    line = lax.broadcasted_iota(jnp.int32, (block.shape[1], spare), 0)
-    packed = jnp.zeros(line.shape, f32)
-    for k, part in enumerate(three_parts(squares)):
-        packed = jnp.where(line == k, part, packed)
+    parts = three_parts(squares)
+    blank = jnp.broadcast_to(0.0 * parts[-1], (block.shape[1] - len(parts), spare))
+    packed = jnp.concatenate(parts + [blank], axis=0)
     packed = jnp.broadcast_to(packed.astype(bf16), (NY,) + packed.shape)
     block = lax.all_to_all(jnp.concatenate([block, packed], axis=2), "y", 0, 0)
     gram = jnp.concatenate([block[y, :, :held] for y in range(NY)], axis=1)

time: 148 us -> 148 us (level)
  blocking collectives: 72.1 us -> 81.2 us
  waiting for transfers between devices: 13.2 us -> 7.19 us
  starting transfers between devices: 33.8 us -> 30 us
    all_to_all x5 -> x6, blocking collectives: 61.6 us -> 70.9 us  [spread(): lax.all_to_all(jnp.broadcast_to(block[None], (size,) + block.shape), axis...]
    all_to_all x2 -> x1, waiting for transfers between devices: 11.5 us -> 5.61 us  [spread(): lax.all_to_all(jnp.broadcast_to(block[None], (size,) + block.shape), axis...]
    all_to_all x2 -> x1, starting transfers between devices: 9.34 us -> 5.28 us  [spread(): lax.all_to_all(jnp.broadcast_to(block[None], (size,) + block.shape), axis...]
  transfers between devices with their start and end apart: 5 -> 4, of which waited for: 4 -> 3; matrix products, arithmetic and copies ran while one was open for 4% -> 5% of each run, Pallas kernels for 0% -> 0%
where the time goes in v7:
time: 148 us; the launch traced here: 147 us
  blocking collectives  81.2 us (55%)
  starting transfers between devices  30 us (20%)
  between operations  14.9 us (10%)
  matrix products  7.41 us (5%)
  waiting for transfers between devices  7.19 us (5%)
  other arithmetic  4.03 us (3%)
  local copies, waits for them, and re-layouts  2.38 us (2%)
    all_to_all x6, blocking collectives, spread(): lax.all_to_all(jnp.broadcast_to(block[None], (size,) + block.shape), axis...  70.9 us
    ppermute x2, starting transfers between devices, swap(): return lax.ppermute(block, 'c', [(0, 1), (1, 0)])  24.6 us
    all_to_all x1, blocking collectives, body(): block = lax.all_to_all(jnp.concatenate([block, packed], axis=2), 'y', 0, 0)  10.2 us
    all_to_all x1, waiting for transfers between devices, spread(): lax.all_to_all(jnp.broadcast_to(block[None], (size,) + block.shape), axis...  5.61 us
    all_to_all x1, starting transfers between devices, spread(): lax.all_to_all(jnp.broadcast_to(block[None], (size,) + block.shape), axis...  5.28 us
    dot_general x4, matrix products, rows_dot_t(): lax.dot_general(rows, matrix, (((1,), (1,)), ((), ())), preferred_element...  4.07 us
    dot_general x3, matrix products, rows_dot(): jnp.dot(rows.astype(jnp.bfloat16), matrix, preferred_element_type=jnp.flo...  3.35 us
  transfers between devices with their start and end apart: 4, of which 3 were waited for; matrix products, arithmetic and copies ran while one was open for 5% of the time, Pallas kernels for 0%

profile of v7, /device:TPU:1, one launch (start us, length us, event | category | flops | bytes accessed | tf_op | source)
XLA Modules:
  0.0 147.1 jit_solution(14037018364915710029)
XLA Ops:
  7.2 0.0 all-gather.2.cloned.1.call-start
  7.2 1.5 %add_convert_fusion = (bf16[2,16,448]{2,1,0:T(8,128)(2,1)S(1)}, f32[2,16,448]{2,1,0:T(8,128)}) fusion(f32[2,16,448]{2,1,0:T(8,128)} %param.3, f32[2,16,448]{2,1,0:T(8,128)} %param.4), kind=kLoop, calls=%fused_computation.26 | loop fusion | flops 71680 | bytes 200704 | tf_op jit(solution)/shard_map/convert_element_type | solution.py:59
  8.7 12.4 %collective-permute-start = (bf16[16,448]{1,0:T(8,128)(2,1)S(1)}, bf16[16,448]{1,0:T(8,128)(2,1)S(1)}, u32[]{:S(2)}, u32[]{:S(2)}) collective-permute-start(bf16[16,448]{1,0:T(8,128)(2,1)S(1)} %get-tuple-element.27), channel_id=1, source_target_pairs={{0,1},{1,0},{2,3},{3,2},{4,5},{5,4},{6,7},{7,6},{8,9},{9,8},{10,11... | collective-permute-start | bytes 43016 | tf_op jit(solution)/shard_map/ppermute | solution.py:39
  21.1 1.3 dynamic_slice.3
  22.4 0.6 iota_compare_fusion
  23.1 0.0 collective-permute-done
  23.1 0.1 maximum_select_fusion
  23.2 22.9 %all_to_all.40 = bf16[12,16,896]{2,1,0:T(8,128)(2,1)} all-to-all(bf16[12,16,896]{2,1,0:T(8,128)(2,1)S(1)} %broadcast_in_dim.29), channel_id=1, replica_groups=mesh['z'=12,'y'=8,'x'=4,'c'=2] {'z'}, dimensions={0} | all-to-all | bytes 688128 | tf_op jit(solution)/shard_map/all_to_all | solution.py:33
  46.1 0.0 all-gather.2.cloned.1.call-update
  46.1 15.7 %all_to_all.41 = bf16[8,16,896]{2,1,0:T(8,128)(2,1)S(1)} all-to-all(bf16[8,16,896]{2,1,0:T(8,128)(2,1)S(1)} %broadcast_in_dim.30), channel_id=1, replica_groups=mesh['z'=12,'y'=8,'x'=4,'c'=2] {'y'}, dimensions={0} | all-to-all | bytes 458752 | tf_op jit(solution)/shard_map/all_to_all | solution.py:33
  61.8 1.2 convolution_convert_fusion.3
  63.1 9.0 %all_to_all.42 = bf16[4,128,192]{1,2,0:T(8,128)(2,1)S(1)} all-to-all(bf16[4,128,192]{1,2,0:T(8,128)(2,1)S(1)} %broadcast_in_dim.31), channel_id=1, replica_groups=mesh['z'=12,'y'=8,'x'=4,'c'=2] {'x'}, dimensions={0} | all-to-all | bytes 393216 | tf_op jit(solution)/shard_map/all_to_all | solution.py:33
  72.2 0.1 fusion.16
  72.3 0.1 copy.17
  72.4 0.1 reduce-precision_convert_fusion.1
  72.6 0.1 pad_maximum_fusion
  72.7 10.2 %all_to_all.43 = bf16[8,16,256]{2,1,0:T(8,128)(2,1)S(1)} all-to-all(bf16[8,16,256]{2,1,0:T(8,128)(2,1)S(1)} %pad_maximum_fusion), channel_id=1, replica_groups=mesh['z'=12,'y'=8,'x'=4,'c'=2] {'y'}, dimensions={0} | all-to-all | bytes 131072 | tf_op jit(solution)/shard_map/all_to_all | solution.py:85
  82.9 0.1 convert_reduce_fusion.4
  83.0 0.6 broadcast_in_dim.73
  83.6 5.3 %all-to-all-start.4 = ((f32[12,1,128]{2,1,0:T(1,128)}), f32[12,1,128]{2,1,0:T(1,128)S(1)}, u32[]{:S(2)}, u32[]{:S(2)}) async-start(f32[12,1,128]{2,1,0:T(1,128)} %broadcast_in_dim.73), calls=%async_computation.4 | async-start | bytes 12288 | tf_op jit(solution)/shard_map/all_to_all | solution.py:33
  88.9 0.1 concatenate.23
  89.0 0.7 all-gather.2.cloned.1.call-done
  89.7 0.0 copy-start
  89.7 2.4 %fusion.17 = f32[16,896]{1,0:T(8,128)S(1)} fusion(bf16[16,1536]{1,0:T(8,128)(2,1)S(1)} %concatenate.23, bf16[1536,896]{1,0:T(8,128)(2,1)} %all-gather.2.cloned.1.call-done), kind=kOutput, calls=%fused_computation.62 | convolution fusion | flops 44040192 | bytes 2859008 | tf_op jit(solution)/shard_map/dot_general | solution.py:53
  92.1 5.6 %all-to-all-done.4 = f32[12,1,128]{2,1,0:T(1,128)S(1)} async-done(((f32[12,1,128]{2,1,0:T(1,128)}), f32[12,1,128]{2,1,0:T(1,128)S(1)}, u32[]{:S(2)}, u32[]{:S(2)}) %all-to-all-start.4) | async-done | bytes 6176 | tf_op jit(solution)/shard_map/all_to_all | solution.py:33
  97.7 0.6 reduce_sum.66
  99.1 0.0 copy-done
  99.1 0.8 convolution_convert_fusion.2
  100.0 7.5 %all_to_all.44 = bf16[4,16,1536]{2,1,0:T(8,128)(2,1)S(1)} all-to-all(bf16[4,16,1536]{2,1,0:T(8,128)(2,1)S(1)} %broadcast_in_dim.74), channel_id=1, replica_groups=mesh['z'=12,'y'=8,'x'=4,'c'=2] {'x'}, dimensions={0} | all-to-all | bytes 393216 | tf_op jit(solution)/shard_map/all_to_all | solution.py:33
  107.5 1.2 convolution_convert_fusion.1
  108.8 7.5 %all_to_all.45 = bf16[4,16,1536]{2,1,0:T(8,128)(2,1)S(1)} all-to-all(bf16[4,16,1536]{2,1,0:T(8,128)(2,1)S(1)} %broadcast_in_dim.75), channel_id=1, replica_groups=mesh['z'=12,'y'=8,'x'=4,'c'=2] {'x'}, dimensions={0} | all-to-all | bytes 393216 | tf_op jit(solution)/shard_map/all_to_all | solution.py:33
  116.4 0.5 convolution_convert_fusion.4
  116.8 0.8 convolution_convert_fusion
  117.7 8.2 %all_to_all.46 = bf16[4,16,1536]{2,1,0:T(8,128)(2,1)S(1)} all-to-all(bf16[4,16,1536]{2,1,0:T(8,128)(2,1)S(1)} %broadcast_in_dim.76), channel_id=1, replica_groups=mesh['z'=12,'y'=8,'x'=4,'c'=2] {'x'}, dimensions={0} | all-to-all | bytes 393216 | tf_op jit(solution)/shard_map/all_to_all | solution.py:33
  125.9 0.5 fusion.5
  126.4 0.1 slice.81
  126.5 12.3 %collective-permute-start.1 = (bf16[16,448]{1,0:T(8,128)(2,1)S(1)}, bf16[16,448]{1,0:T(8,128)(2,1)S(1)}, u32[]{:S(2)}, u32[]{:S(2)}) collective-permute-start(bf16[16,448]{1,0:T(8,128)(2,1)S(1)} %slice.81), channel_id=1, source_target_pairs={{0,1},{1,0},{2,3},{3,2},{4,5},{5,4},{6,7},{7,6},{8,9},{9,8},{10,11... | collective-permute-start | bytes 43016 | tf_op jit(solution)/shard_map/ppermute | solution.py:39
  138.8 0.8 collective-permute-done.1
  139.6 0.6 convert_multiply_fusion.2
  (19 shorter events, 0.4 us)
Async XLA Ops:
  7.2 82.6 %all-gather.2.cloned.1.call-start = ((), (), s32[]{:S(2)}) async-start(), calls=%async_computation.8 | async-start | bytes 3096576 | tf_op jit(solution)/shard_map/all_gather | solution.py:71
  8.7 14.3 %collective-permute-start = (bf16[16,448]{1,0:T(8,128)(2,1)S(1)}, bf16[16,448]{1,0:T(8,128)(2,1)S(1)}, u32[]{:S(2)}, u32[]{:S(2)}) collective-permute-start(bf16[16,448]{1,0:T(8,128)(2,1)S(1)} %get-tuple-element.27), channel_id=1, source_target_pairs={{0,1},{1,0},{2,3},{3,2},{4,5},{5,4},{6,7},{7,6},{8,9},{9,8},{10,11... | collective-permute-start | bytes 43016 | tf_op jit(solution)/shard_map/ppermute | solution.py:39
  83.6 14.2 %all-to-all-start.4 = ((f32[12,1,128]{2,1,0:T(1,128)}), f32[12,1,128]{2,1,0:T(1,128)S(1)}, u32[]{:S(2)}, u32[]{:S(2)}) async-start(f32[12,1,128]{2,1,0:T(1,128)} %broadcast_in_dim.73), calls=%async_computation.4 | async-start | bytes 12288 | tf_op jit(solution)/shard_map/all_to_all | solution.py:33
  89.7 9.4 %copy-start = (bf16[1536,896]{1,0:T(8,128)(2,1)S(1)}, bf16[1536,896]{1,0:T(8,128)(2,1)}, u32[]{:S(2)}) copy-start(bf16[1536,896]{1,0:T(8,128)(2,1)} %all-gather.2.cloned.1.call-done) | copy-start | bytes 8257540
  126.5 13.1 %collective-permute-start.1 = (bf16[16,448]{1,0:T(8,128)(2,1)S(1)}, bf16[16,448]{1,0:T(8,128)(2,1)S(1)}, u32[]{:S(2)}, u32[]{:S(2)}) collective-permute-start(bf16[16,448]{1,0:T(8,128)(2,1)S(1)} %slice.81), channel_id=1, source_target_pairs={{0,1},{1,0},{2,3},{3,2},{4,5},{5,4},{6,7},{7,6},{8,9},{9,8},{10,11... | collective-permute-start | bytes 43016 | tf_op jit(solution)/shard_map/ppermute | solution.py:39
Sparse Core Ops, SparseCore 0:
  46.2 43.4 all-gather.1

commit v8 on v7

--- a/solution.py
+++ b/solution.py
@@ -67,25 +67,24 @@
     own_length = lax.dynamic_slice(lengths, (core, dp), (1, 1))
     slots = lax.broadcasted_iota(jnp.int32, rows.shape, 0)
     rows = jnp.where(slots < own_length, rows, jnp.zeros_like(rows))
-    same_y = spread(rows, "z", NZ).reshape(-1, columns)
-    matrix = lax.all_gather(same_y, "y", axis=0, tiled=True)
+    same_z = spread(rows, "y", NY).reshape(-1, columns)
+    matrix = lax.all_gather(same_z, "z", axis=0, tiled=True)
 
-    rows_later, same_y = lax.optimization_barrier((rows, same_y))
-    same_z = spread(rows_later, "y", NY).reshape(-1, columns)
-    block = sum_columns(rows_dot_t(same_z, same_y))
+    rows_later, same_z = lax.optimization_barrier((rows, same_z))
+    same_y = spread(rows_later, "z", NZ).reshape(-1, columns)
+    block = sum_columns(rows_dot_t(same_y, same_z))
     squares = jnp.sum(block * block, axis=0, keepdims=True)
-    block = block.astype(bf16).reshape(NY, -1, block.shape[1])
+    block = block.astype(bf16).reshape(NZ, -1, block.shape[1])
     held = block.shape[2]
     spare = PACKED - held
-    squares = sum(squares[:, k : k + spare] for k in range(0, held, spare))
     parts = three_parts(squares)
     blank = jnp.broadcast_to(0.0 * parts[-1], (block.shape[1] - len(parts), spare))
     packed = jnp.concatenate(parts + [blank], axis=0)
-    packed = jnp.broadcast_to(packed.astype(bf16), (NY,) + packed.shape)
-    block = lax.all_to_all(jnp.concatenate([block, packed], axis=2), "y", 0, 0)
-    gram = jnp.concatenate([block[y, :, :held] for y in range(NY)], axis=1)
+    packed = jnp.broadcast_to(packed.astype(bf16), (NZ,) + packed.shape)
+    block = lax.all_to_all(jnp.concatenate([block, packed], axis=2), "z", 0, 0)
+    gram = jnp.concatenate([block[z, :, :held] for z in range(NZ)], axis=1)
     squares = jnp.sum(block[:, :, held:].astype(f32), axis=(0, 1))[None]
-    squares = spread(jnp.concatenate([squares, jnp.zeros_like(squares)], axis=1), "z", NZ)
+    squares = spread(squares, "y", NY)
     product = rows_dot(gram, matrix)
     product, squares = lax.optimization_barrier((product, squares))
     total_sq = jnp.sum(squares)

time: 148 us -> 160 us (1.081)
  waiting for transfers between devices: 7.19 us -> 28 us
  blocking collectives: 81.2 us -> 65 us
  starting transfers between devices: 30 us -> 37.6 us
    all_to_all x6 -> x5, blocking collectives: 70.9 us -> 49.5 us  [spread(): lax.all_to_all(jnp.broadcast_to(block[None], (size,) + block.shape), axis...]
    all_to_all x1 -> x2, waiting for transfers between devices: 5.61 us -> 16.6 us  [spread(): lax.all_to_all(jnp.broadcast_to(block[None], (size,) + block.shape), axis...]
    all_gather x1, waiting for transfers between devices: 0.74 us -> 9.92 us  [body(): matrix = lax.all_gather(same_z, 'z', axis=0, tiled=True)]
    all_to_all x1 -> x2, starting transfers between devices: 5.28 us -> 12.8 us  [spread(): lax.all_to_all(jnp.broadcast_to(block[None], (size,) + block.shape), axis...]
    all_to_all x1, blocking collectives: 10.2 us -> 15.5 us  [body(): block = lax.all_to_all(jnp.concatenate([block, packed], axis=2), 'z', 0, 0)]
  transfers between devices with their start and end apart: 4 -> 5, of which waited for: 3 -> 3; matrix products, arithmetic and copies ran while one was open for 5% -> 4% of each run, Pallas kernels for 0% -> 0%
where the time goes in v8:
time: 160 us
  blocking collectives  65 us (41%)
  starting transfers between devices  37.6 us (24%)
  waiting for transfers between devices  28 us (18%)
  between operations  15 us (9%)
  matrix products  7.35 us (5%)
  other arithmetic  3.78 us (2%)
  local copies, waits for them, and re-layouts  3 us (2%)
    all_to_all x5, blocking collectives, spread(): lax.all_to_all(jnp.broadcast_to(block[None], (size,) + block.shape), axis...  49.5 us
    ppermute x2, starting transfers between devices, swap(): return lax.ppermute(block, 'c', [(0, 1), (1, 0)])  24.8 us
    all_to_all x2, waiting for transfers between devices, spread(): lax.all_to_all(jnp.broadcast_to(block[None], (size,) + block.shape), axis...  16.6 us
    all_to_all x1, blocking collectives, body(): block = lax.all_to_all(jnp.concatenate([block, packed], axis=2), 'z', 0, 0)  15.5 us
    all_to_all x2, starting transfers between devices, spread(): lax.all_to_all(jnp.broadcast_to(block[None], (size,) + block.shape), axis...  12.8 us
    all_gather x1, waiting for transfers between devices, body(): matrix = lax.all_gather(same_z, 'z', axis=0, tiled=True)  9.92 us
    dot_general x4, matrix products, rows_dot_t(): lax.dot_general(rows, matrix, (((1,), (1,)), ((), ())), preferred_element...  4.01 us
    dot_general x3, matrix products, rows_dot(): jnp.dot(rows.astype(jnp.bfloat16), matrix, preferred_element_type=jnp.flo...  3.35 us
  transfers between devices with their start and end apart: 5, of which 3 were waited for; matrix products, arithmetic and copies ran while one was open for 4% of the time, Pallas kernels for 0%

profile of v8, /device:TPU:1, one launch (start us, length us, event | category | flops | bytes accessed | tf_op | source)
XLA Modules:
  0.0 159.8 jit_solution(12329332817806332641)
XLA Ops:
  7.2 1.5 add_convert_fusion
  8.7 12.4 %collective-permute-start = (bf16[16,448]{1,0:T(8,128)(2,1)S(1)}, bf16[16,448]{1,0:T(8,128)(2,1)S(1)}, u32[]{:S(2)}, u32[]{:S(2)}) collective-permute-start(bf16[16,448]{1,0:T(8,128)(2,1)S(1)} %get-tuple-element.17), channel_id=1, source_target_pairs={{0,1},{1,0},{2,3},{3,2},{4,5},{5,4},{6,7},{7,6},{8,9},{9,8},{10,11... | collective-permute-start | bytes 43016 | tf_op jit(solution)/shard_map/ppermute | solution.py:39
  21.1 1.3 dynamic_slice.3
  22.4 0.6 iota_compare_fusion
  23.0 0.0 collective-permute-done
  23.0 0.1 maximum_select_fusion
  23.1 14.8 %all_to_all.40 = bf16[8,16,896]{2,1,0:T(8,128)(2,1)} all-to-all(bf16[8,16,896]{2,1,0:T(8,128)(2,1)S(1)} %broadcast_in_dim.21), channel_id=1, replica_groups=mesh['z'=12,'y'=8,'x'=4,'c'=2] {'y'}, dimensions={0} | all-to-all | bytes 458752 | tf_op jit(solution)/shard_map/all_to_all | solution.py:33
  37.9 0.8 broadcast_in_dim.22
  38.7 9.5 %all-to-all-start.1 = ((bf16[12,16,896]{2,1,0:T(8,128)(2,1)}), bf16[12,16,896]{2,1,0:T(8,128)(2,1)S(1)}, u32[]{:S(2)}, u32[]{:S(2)}) async-start(bf16[12,16,896]{2,1,0:T(8,128)(2,1)} %broadcast_in_dim.22), calls=%async_computation.1 | async-start | bytes 688128 | tf_op jit(solution)/shard_map/all_to_all | solution.py:33
  48.1 0.0 all-gather.2.cloned.1.call-start
  48.2 0.7 all-gather.2.cloned.1.call-update
  48.9 16.6 %all-to-all-done.1 = bf16[12,16,896]{2,1,0:T(8,128)(2,1)S(1)} async-done(((bf16[12,16,896]{2,1,0:T(8,128)(2,1)}), bf16[12,16,896]{2,1,0:T(8,128)(2,1)S(1)}, u32[]{:S(2)}, u32[]{:S(2)}) %all-to-all-start.1) | async-done | bytes 344096 | tf_op jit(solution)/shard_map/all_to_all | solution.py:33
  65.4 1.2 convolution_convert_fusion.3
  66.7 9.1 %all_to_all.41 = bf16[4,192,128]{2,1,0:T(8,128)(2,1)S(1)} all-to-all(bf16[4,192,128]{2,1,0:T(8,128)(2,1)S(1)} %broadcast_in_dim.23), channel_id=1, replica_groups=mesh['z'=12,'y'=8,'x'=4,'c'=2] {'x'}, dimensions={0} | all-to-all | bytes 393216 | tf_op jit(solution)/shard_map/all_to_all | solution.py:33
  75.9 15.5 %all_to_all.42 = bf16[12,16,256]{2,1,0:T(8,128)(2,1)S(1)} all-to-all(bf16[12,16,256]{2,1,0:T(8,128)(2,1)S(1)} %pad_maximum_fusion), channel_id=1, replica_groups=mesh['z'=12,'y'=8,'x'=4,'c'=2] {'z'}, dimensions={0} | all-to-all | bytes 196608 | tf_op jit(solution)/shard_map/all_to_all | solution.py:84
  91.4 0.6 broadcast_in_dim.26
  92.0 3.3 %all-to-all-start.4 = ((f32[8,1,128]{2,1,0:T(1,128)}), f32[8,1,128]{2,1,0:T(1,128)S(1)}, u32[]{:S(2)}, u32[]{:S(2)}) async-start(f32[8,1,128]{2,1,0:T(1,128)} %broadcast_in_dim.26), calls=%async_computation.4 | async-start | bytes 8192 | tf_op jit(solution)/shard_map/all_to_all | solution.py:33
  95.5 9.9 %all-gather.2.cloned.1.call-done = bf16[1536,896]{1,0:T(8,128)(2,1)} async-done(((bf16[128,896]{1,0:T(8,128)(2,1)}), bf16[1536,896]{1,0:T(8,128)(2,1)}) %all-gather.2.cloned.1.call-update) | async-done | bytes 2752528 | tf_op jit(solution)/shard_map/all_gather | solution.py:71
  105.4 0.0 copy-start
  105.4 2.4 %fusion.20 = f32[16,896]{1,0:T(8,128)S(1)} fusion(bf16[16,1536]{1,0:T(8,128)(2,1)S(1)} %constant_dynamic-update-slice_fusion, bf16[1536,896]{1,0:T(8,128)(2,1)} %all-gather.2.cloned.1.call-done), kind=kOutput, calls=%fused_computation.79 | convolution fusion | flops 44040192 | bytes 2859008 | tf_op jit(solution)/shard_map/dot_general | solution.py:53
  107.8 0.0 all-to-all-done.4
  107.8 0.6 reduce_sum.69
  109.2 0.0 copy-done
  109.2 0.8 convolution_convert_fusion.2
  110.1 9.3 %all_to_all.43 = bf16[4,16,1536]{2,1,0:T(8,128)(2,1)S(1)} all-to-all(bf16[4,16,1536]{2,1,0:T(8,128)(2,1)S(1)} %broadcast_in_dim.27), channel_id=1, replica_groups=mesh['z'=12,'y'=8,'x'=4,'c'=2] {'x'}, dimensions={0} | all-to-all | bytes 393216 | tf_op jit(solution)/shard_map/all_to_all | solution.py:33
  119.4 1.2 convolution_convert_fusion.1
  120.6 7.6 %all_to_all.44 = bf16[4,16,1536]{2,1,0:T(8,128)(2,1)S(1)} all-to-all(bf16[4,16,1536]{2,1,0:T(8,128)(2,1)S(1)} %broadcast_in_dim.28), channel_id=1, replica_groups=mesh['z'=12,'y'=8,'x'=4,'c'=2] {'x'}, dimensions={0} | all-to-all | bytes 393216 | tf_op jit(solution)/shard_map/all_to_all | solution.py:33
  128.2 0.5 convolution_convert_fusion.4
  128.7 0.8 convolution_convert_fusion
  129.6 8.8 %all_to_all.45 = bf16[4,16,1536]{2,1,0:T(8,128)(2,1)S(1)} all-to-all(bf16[4,16,1536]{2,1,0:T(8,128)(2,1)S(1)} %broadcast_in_dim.29), channel_id=1, replica_groups=mesh['z'=12,'y'=8,'x'=4,'c'=2] {'x'}, dimensions={0} | all-to-all | bytes 393216 | tf_op jit(solution)/shard_map/all_to_all | solution.py:33
  138.4 0.5 fusion.5
  138.9 0.1 slice.86
  139.0 12.5 %collective-permute-start.1 = (bf16[16,448]{1,0:T(8,128)(2,1)S(1)}, bf16[16,448]{1,0:T(8,128)(2,1)S(1)}, u32[]{:S(2)}, u32[]{:S(2)}) collective-permute-start(bf16[16,448]{1,0:T(8,128)(2,1)S(1)} %slice.86), channel_id=1, source_target_pairs={{0,1},{1,0},{2,3},{3,2},{4,5},{5,4},{6,7},{7,6},{8,9},{9,8},{10,11... | collective-permute-start | bytes 43016 | tf_op jit(solution)/shard_map/ppermute | solution.py:39
  151.5 0.8 collective-permute-done.1
  152.3 0.6 convert_multiply_fusion.2
  (32 shorter events, 0.5 us)
Async XLA Ops:
  8.7 14.3 %collective-permute-start = (bf16[16,448]{1,0:T(8,128)(2,1)S(1)}, bf16[16,448]{1,0:T(8,128)(2,1)S(1)}, u32[]{:S(2)}, u32[]{:S(2)}) collective-permute-start(bf16[16,448]{1,0:T(8,128)(2,1)S(1)} %get-tuple-element.17), channel_id=1, source_target_pairs={{0,1},{1,0},{2,3},{3,2},{4,5},{5,4},{6,7},{7,6},{8,9},{9,8},{10,11... | collective-permute-start | bytes 43016 | tf_op jit(solution)/shard_map/ppermute | solution.py:39
  38.7 26.8 %all-to-all-start.1 = ((bf16[12,16,896]{2,1,0:T(8,128)(2,1)}), bf16[12,16,896]{2,1,0:T(8,128)(2,1)S(1)}, u32[]{:S(2)}, u32[]{:S(2)}) async-start(bf16[12,16,896]{2,1,0:T(8,128)(2,1)} %broadcast_in_dim.22), calls=%async_computation.1 | async-start | bytes 688128 | tf_op jit(solution)/shard_map/all_to_all | solution.py:33
  48.1 57.3 %all-gather.2.cloned.1.call-start = ((), (), s32[]{:S(2)}) async-start(), calls=%async_computation.8 | async-start | bytes 2981888 | tf_op jit(solution)/shard_map/all_gather | solution.py:71
  92.0 15.8 %all-to-all-start.4 = ((f32[8,1,128]{2,1,0:T(1,128)}), f32[8,1,128]{2,1,0:T(1,128)S(1)}, u32[]{:S(2)}, u32[]{:S(2)}) async-start(f32[8,1,128]{2,1,0:T(1,128)} %broadcast_in_dim.26), calls=%async_computation.4 | async-start | bytes 8192 | tf_op jit(solution)/shard_map/all_to_all | solution.py:33
  105.4 3.8 %copy-start = (bf16[1536,896]{1,0:T(8,128)(2,1)S(1)}, bf16[1536,896]{1,0:T(8,128)(2,1)}, u32[]{:S(2)}) copy-start(bf16[1536,896]{1,0:T(8,128)(2,1)} %all-gather.2.cloned.1.call-done) | copy-start | bytes 8257540
  139.0 13.3 %collective-permute-start.1 = (bf16[16,448]{1,0:T(8,128)(2,1)S(1)}, bf16[16,448]{1,0:T(8,128)(2,1)S(1)}, u32[]{:S(2)}, u32[]{:S(2)}) collective-permute-start(bf16[16,448]{1,0:T(8,128)(2,1)S(1)} %slice.86), channel_id=1, source_target_pairs={{0,1},{1,0},{2,3},{3,2},{4,5},{5,4},{6,7},{7,6},{8,9},{9,8},{10,11... | collective-permute-start | bytes 43016 | tf_op jit(solution)/shard_map/ppermute | solution.py:39
Sparse Core Ops, SparseCore 0:
  51.3 54.0 all-gather.1

commit v9 on v7

--- a/solution.py
+++ b/solution.py
@@ -55,8 +55,7 @@
 
 def body(grad, momentum, lengths):
     f32, bf16 = jnp.float32, jnp.bfloat16
-    new_momentum = MOMENTUM_COEF * momentum + grad
-    rounded = (grad + MOMENTUM_COEF * new_momentum).astype(bf16)
+    rounded = (grad + MOMENTUM_COEF * (MOMENTUM_COEF * momentum + grad)).astype(bf16)
     dp = lax.axis_index("z") * NY + lax.axis_index("y")
     core = lax.axis_index("c")
     first_core = core == 0
@@ -70,7 +69,8 @@
     same_y = spread(rows, "z", NZ).reshape(-1, columns)
     matrix = lax.all_gather(same_y, "y", axis=0, tiled=True)
 
-    rows_later, same_y = lax.optimization_barrier((rows, same_y))
+    rows_later, same_y, grad, momentum = lax.optimization_barrier((rows, same_y, grad, momentum))
+    new_momentum = MOMENTUM_COEF * momentum + grad
     same_z = spread(rows_later, "y", NY).reshape(-1, columns)
     block = sum_columns(rows_dot_t(same_z, same_y))
     squares = jnp.sum(block * block, axis=0, keepdims=True)

time: 148 us -> 147 us (level)
  no operation moved by 1% of the time
where the time goes in v9:
time: 147 us
  blocking collectives  81.2 us (55%)
  starting transfers between devices  30 us (20%)
  between operations  15 us (10%)
  matrix products  7.41 us (5%)
  waiting for transfers between devices  6.53 us (4%)
  other arithmetic  4.05 us (3%)
  local copies, waits for them, and re-layouts  2.38 us (2%)
    all_to_all x6, blocking collectives, spread(): lax.all_to_all(jnp.broadcast_to(block[None], (size,) + block.shape), axis...  71 us
    ppermute x2, starting transfers between devices, swap(): return lax.ppermute(block, 'c', [(0, 1), (1, 0)])  24.7 us
    all_to_all x1, blocking collectives, body(): block = lax.all_to_all(jnp.concatenate([block, packed], axis=2), 'y', 0, 0)  10.2 us
    all_to_all x1, waiting for transfers between devices, spread(): lax.all_to_all(jnp.broadcast_to(block[None], (size,) + block.shape), axis...  5.52 us
    all_to_all x1, starting transfers between devices, spread(): lax.all_to_all(jnp.broadcast_to(block[None], (size,) + block.shape), axis...  5.26 us
    dot_general x4, matrix products, rows_dot_t(): lax.dot_general(rows, matrix, (((1,), (1,)), ((), ())), preferred_element...  4.06 us
    dot_general x3, matrix products, rows_dot(): jnp.dot(rows.astype(jnp.bfloat16), matrix, preferred_element_type=jnp.flo...  3.35 us
  transfers between devices with their start and end apart: 4, of which 3 were waited for; matrix products, arithmetic and copies ran while one was open for 5% of the time, Pallas kernels for 0%

profile of v9, /device:TPU:1, one launch (start us, length us, event | category | flops | bytes accessed | tf_op | source)
XLA Modules:
  0.0 146.5 jit_solution(5304398442722660018)
XLA Ops:
  7.2 0.0 all-gather.2.cloned.1.call-start
  7.2 0.9 add_convert_fusion
  8.1 12.4 %collective-permute-start = (bf16[16,448]{1,0:T(8,128)(2,1)S(1)}, bf16[16,448]{1,0:T(8,128)(2,1)S(1)}, u32[]{:S(2)}, u32[]{:S(2)}) collective-permute-start(bf16[16,448]{1,0:T(8,128)(2,1)S(1)} %get-tuple-element.29), channel_id=1, source_target_pairs={{0,1},{1,0},{2,3},{3,2},{4,5},{5,4},{6,7},{7,6},{8,9},{9,8},{10,11... | collective-permute-start | bytes 43016 | tf_op jit(solution)/shard_map/ppermute | solution.py:39
  20.5 1.3 dynamic_slice.3
  21.8 0.6 iota_compare_fusion
  22.4 0.0 collective-permute-done
  22.5 0.1 maximum_select_fusion
  22.6 22.9 %all_to_all.40 = bf16[12,16,896]{2,1,0:T(8,128)(2,1)} all-to-all(bf16[12,16,896]{2,1,0:T(8,128)(2,1)S(1)} %broadcast_in_dim.29), channel_id=1, replica_groups=mesh['z'=12,'y'=8,'x'=4,'c'=2] {'z'}, dimensions={0} | all-to-all | bytes 688128 | tf_op jit(solution)/shard_map/all_to_all | solution.py:33
  45.5 0.0 all-gather.2.cloned.1.call-update
  45.5 15.7 %all_to_all.41 = bf16[8,16,896]{2,1,0:T(8,128)(2,1)S(1)} all-to-all(bf16[8,16,896]{2,1,0:T(8,128)(2,1)S(1)} %broadcast_in_dim.30), channel_id=1, replica_groups=mesh['z'=12,'y'=8,'x'=4,'c'=2] {'y'}, dimensions={0} | all-to-all | bytes 458752 | tf_op jit(solution)/shard_map/all_to_all | solution.py:33
  61.2 1.2 convolution_convert_fusion.3
  62.5 9.1 %all_to_all.42 = bf16[4,128,192]{1,2,0:T(8,128)(2,1)S(1)} all-to-all(bf16[4,128,192]{1,2,0:T(8,128)(2,1)S(1)} %broadcast_in_dim.31), channel_id=1, replica_groups=mesh['z'=12,'y'=8,'x'=4,'c'=2] {'x'}, dimensions={0} | all-to-all | bytes 393216 | tf_op jit(solution)/shard_map/all_to_all | solution.py:33
  71.6 0.1 fusion.16
  71.7 0.1 copy.17
  71.8 0.1 reduce-precision_convert_fusion.1
  72.0 0.1 pad_maximum_fusion
  72.0 10.2 %all_to_all.43 = bf16[8,16,256]{2,1,0:T(8,128)(2,1)S(1)} all-to-all(bf16[8,16,256]{2,1,0:T(8,128)(2,1)S(1)} %pad_maximum_fusion), channel_id=1, replica_groups=mesh['z'=12,'y'=8,'x'=4,'c'=2] {'y'}, dimensions={0} | all-to-all | bytes 131072 | tf_op jit(solution)/shard_map/all_to_all | solution.py:85
  82.3 0.1 convert_reduce_fusion.4
  82.4 0.6 broadcast_in_dim.73
  83.0 5.3 %all-to-all-start.4 = ((f32[12,1,128]{2,1,0:T(1,128)}), f32[12,1,128]{2,1,0:T(1,128)S(1)}, u32[]{:S(2)}, u32[]{:S(2)}) async-start(f32[12,1,128]{2,1,0:T(1,128)} %broadcast_in_dim.73), calls=%async_computation.4 | async-start | bytes 12288 | tf_op jit(solution)/shard_map/all_to_all | solution.py:33
  88.3 0.1 concatenate.23
  88.4 0.8 all-gather.2.cloned.1.call-done
  89.2 0.0 copy-start
  89.2 2.4 %fusion.17 = f32[16,896]{1,0:T(8,128)S(1)} fusion(bf16[16,1536]{1,0:T(8,128)(2,1)S(1)} %concatenate.23, bf16[1536,896]{1,0:T(8,128)(2,1)} %all-gather.2.cloned.1.call-done), kind=kOutput, calls=%fused_computation.62 | convolution fusion | flops 44040192 | bytes 2859008 | tf_op jit(solution)/shard_map/dot_general | solution.py:53
  91.6 5.5 %all-to-all-done.4 = f32[12,1,128]{2,1,0:T(1,128)S(1)} async-done(((f32[12,1,128]{2,1,0:T(1,128)}), f32[12,1,128]{2,1,0:T(1,128)S(1)}, u32[]{:S(2)}, u32[]{:S(2)}) %all-to-all-start.4) | async-done | bytes 6176 | tf_op jit(solution)/shard_map/all_to_all | solution.py:33
  97.1 0.6 reduce_sum.66
  98.5 0.0 copy-done
  98.5 0.8 convolution_convert_fusion.2
  99.4 7.5 %all_to_all.44 = bf16[4,16,1536]{2,1,0:T(8,128)(2,1)S(1)} all-to-all(bf16[4,16,1536]{2,1,0:T(8,128)(2,1)S(1)} %broadcast_in_dim.74), channel_id=1, replica_groups=mesh['z'=12,'y'=8,'x'=4,'c'=2] {'x'}, dimensions={0} | all-to-all | bytes 393216 | tf_op jit(solution)/shard_map/all_to_all | solution.py:33
  106.9 1.2 convolution_convert_fusion.1
  108.2 7.5 %all_to_all.45 = bf16[4,16,1536]{2,1,0:T(8,128)(2,1)S(1)} all-to-all(bf16[4,16,1536]{2,1,0:T(8,128)(2,1)S(1)} %broadcast_in_dim.75), channel_id=1, replica_groups=mesh['z'=12,'y'=8,'x'=4,'c'=2] {'x'}, dimensions={0} | all-to-all | bytes 393216 | tf_op jit(solution)/shard_map/all_to_all | solution.py:33
  115.7 0.5 convolution_convert_fusion.4
  116.2 0.0 copy-start.1
  116.2 0.0 copy-start.2
  116.2 0.8 convolution_convert_fusion
  117.1 8.2 %all_to_all.46 = bf16[4,16,1536]{2,1,0:T(8,128)(2,1)S(1)} all-to-all(bf16[4,16,1536]{2,1,0:T(8,128)(2,1)S(1)} %broadcast_in_dim.76), channel_id=1, replica_groups=mesh['z'=12,'y'=8,'x'=4,'c'=2] {'x'}, dimensions={0} | all-to-all | bytes 393216 | tf_op jit(solution)/shard_map/all_to_all | solution.py:33
  125.3 0.5 fusion.5
  125.8 0.1 slice.81
  125.9 12.3 %collective-permute-start.1 = (bf16[16,448]{1,0:T(8,128)(2,1)S(1)}, bf16[16,448]{1,0:T(8,128)(2,1)S(1)}, u32[]{:S(2)}, u32[]{:S(2)}) collective-permute-start(bf16[16,448]{1,0:T(8,128)(2,1)S(1)} %slice.81), channel_id=1, source_target_pairs={{0,1},{1,0},{2,3},{3,2},{4,5},{5,4},{6,7},{7,6},{8,9},{9,8},{10,11... | collective-permute-start | bytes 43016 | tf_op jit(solution)/shard_map/ppermute | solution.py:39
  138.2 0.0 copy-done.1
  138.2 0.0 copy-done.2
  138.2 0.6 multiply_add_fusion
  138.9 0.2 collective-permute-done.1
  139.0 0.6 convert_multiply_fusion.2
  (19 shorter events, 0.4 us)
Async XLA Ops:
  7.2 82.0 %all-gather.2.cloned.1.call-start = ((), (), s32[]{:S(2)}) async-start(), calls=%async_computation.8 | async-start | bytes 3096576 | tf_op jit(solution)/shard_map/all_gather | solution.py:70
  8.1 14.3 %collective-permute-start = (bf16[16,448]{1,0:T(8,128)(2,1)S(1)}, bf16[16,448]{1,0:T(8,128)(2,1)S(1)}, u32[]{:S(2)}, u32[]{:S(2)}) collective-permute-start(bf16[16,448]{1,0:T(8,128)(2,1)S(1)} %get-tuple-element.29), channel_id=1, source_target_pairs={{0,1},{1,0},{2,3},{3,2},{4,5},{5,4},{6,7},{7,6},{8,9},{9,8},{10,11... | collective-permute-start | bytes 43016 | tf_op jit(solution)/shard_map/ppermute | solution.py:39
  83.0 14.1 %all-to-all-start.4 = ((f32[12,1,128]{2,1,0:T(1,128)}), f32[12,1,128]{2,1,0:T(1,128)S(1)}, u32[]{:S(2)}, u32[]{:S(2)}) async-start(f32[12,1,128]{2,1,0:T(1,128)} %broadcast_in_dim.73), calls=%async_computation.4 | async-start | bytes 12288 | tf_op jit(solution)/shard_map/all_to_all | solution.py:33
  89.2 9.3 %copy-start = (bf16[1536,896]{1,0:T(8,128)(2,1)S(1)}, bf16[1536,896]{1,0:T(8,128)(2,1)}, u32[]{:S(2)}) copy-start(bf16[1536,896]{1,0:T(8,128)(2,1)} %all-gather.2.cloned.1.call-done) | copy-start | bytes 8257540
  116.2 22.0 %copy-start.1 = (f32[2,16,448]{2,1,0:T(8,128)S(1)}, f32[2,16,448]{2,1,0:T(8,128)}, u32[]{:S(2)}) copy-start(f32[2,16,448]{2,1,0:T(8,128)} %param.3) | copy-start | bytes 172036
  116.2 22.0 %copy-start.2 = (f32[2,16,448]{2,1,0:T(8,128)S(1)}, f32[2,16,448]{2,1,0:T(8,128)}, u32[]{:S(2)}) copy-start(f32[2,16,448]{2,1,0:T(8,128)} %param.4) | copy-start | bytes 172036
  125.9 13.1 %collective-permute-start.1 = (bf16[16,448]{1,0:T(8,128)(2,1)S(1)}, bf16[16,448]{1,0:T(8,128)(2,1)S(1)}, u32[]{:S(2)}, u32[]{:S(2)}) collective-permute-start(bf16[16,448]{1,0:T(8,128)(2,1)S(1)} %slice.81), channel_id=1, source_target_pairs={{0,1},{1,0},{2,3},{3,2},{4,5},{5,4},{6,7},{7,6},{8,9},{9,8},{10,11... | collective-permute-start | bytes 43016 | tf_op jit(solution)/shard_map/ppermute | solution.py:39
Sparse Core Ops, SparseCore 0:
  45.6 43.5 all-gather.1
